TPU v7x, 128 devices: a whole 4x4x4 slice. The times are simulated.
128 devices in a mesh: req: 32 (over y, x, core), kv: 4 (over z).
Axes of the slice: x: 4, y: 4, z: 4, core: 2. Of those that a mesh axis runs over, the one named last changes fastest.
Arguments:
- tokens: bfloat16 [4096, 2048], P('req'), may hold values from -6 to 6
- lengths: int32 [4096], replicated, may hold values from 1 to 1024, as said below
- page_table: int32 [4096, 16], P('req'), may hold values from 0 to 367, as said below
- key_cache: bfloat16 [11776, 4, 64, 128], P('req', 'kv'), may hold values from -320 to 320
- value_page_cache: bfloat16 [11776, 4, 64, 128], P('req', 'kv'), may hold values from -6 to 6
- mig_slot: int32 [32, 2], replicated, may hold values from 0 to 127, as said below
- attn_gain: float32 [2048], replicated, may hold values from 0.1 to 1.9
- w_query: bfloat16 [2048, 4096], P(None, 'kv'), may hold values from -0.125 to 0.125
- key_weight: bfloat16 [2048, 512], P(None, 'kv'), may hold values from -0.125 to 0.125
- value_weight: bfloat16 [2048, 512], P(None, 'kv'), may hold values from -0.125 to 0.125
- w_out: bfloat16 [4096, 2048], P('kv'), may hold values from -0.09375 to 0.09375
- moe_gain: float32 [2048], replicated, may hold values from 0.1 to 1.9
- routes: int32 [4096, 8], P(('req', 'kv')), may hold values from 0 to 127, all different within a row; in each aligned block of 32 rows (0 to 31, 32 to 63, ...) at most 4 rows name the same one
- gate_probs: float32 [4096, 8], P(('req', 'kv')), may hold values from 0.05 to 1
- w_gate: bfloat16 [128, 2048, 768], P(('req', 'kv')), may hold values from -0.125 to 0.125
- w_up: bfloat16 [128, 2048, 768], P(('req', 'kv')), may hold values from -0.125 to 0.125
- w_down: bfloat16 [128, 768, 2048], P(('req', 'kv')), may hold values from -0.21875 to 0.21875
Outputs:
- layer_out: bfloat16 [4096, 2048], P(('req', 'kv'))
- moved_keys: bfloat16 [64, 4, 1024, 128], P('req', 'kv')
- moved_values: bfloat16 [64, 4, 1024, 128], P('req', 'kv')
Inputs may be any that keep to these rules, and one draw needn't show every extreme that they name: `lengths`: in each block of 128 requests of one index of req, between 2 and 16 requests are longer than 64 tokens and the others are at most 64 long; some request is exactly 1024 long. `page_table`: entries j below the ceiling of lengths[r] / 64 name distinct pages of the pool of request r's own index of req, counted within that pool; later entries are arbitrary pages of that pool. `mig_slot`: row g names 2 distinct local rows of index g of req, each a request longer than 64 tokens. `routes`: in the rows of one device (aligned blocks of 32 rows) no expert is named by more than 4 rows.
All inputs are finite; a program needn't handle non-finite values.
Results may differ from a plain program's by a relative error of at most 0.011.
Values may be sent and summed in bfloat16 or wider, within the bound.
No kernel may reach another device: no remote copies, remote signals or barrier semaphores. Data moves between devices by JAX's collectives and lax.ppermute only.
A program may use at most 128 MiB of HBM per device.

v0:
```python
import math

import jax
import jax.numpy as jnp
from jax import lax
from jax.sharding import PartitionSpec as P

EPSILON = 1e-06
THETA = 1000000.0


def from_behind(shard, axis, by):
    size = lax.axis_size(axis)
    return lax.ppermute(shard, axis, [(i, (i + by) % size) for i in range(size)])


def rms_scale(inputs, gain_vec):
    return (
        inputs * lax.rsqrt(jnp.mean(inputs * inputs, axis=-1, keepdims=True) + EPSILON) * gain_vec
    )


def rotate(vectors, positions):
    half_width = vectors.shape[-1] // 2
    exponent = jnp.arange(half_width, dtype=jnp.float32) * (-2.0 / vectors.shape[-1])
    angles = positions.astype(jnp.float32)[..., None] * THETA**exponent
    cosine = jnp.cos(angles)
    sine_part = jnp.sin(angles)
    front_half = vectors[..., :half_width]
    back_half = vectors[..., half_width:]
    return jnp.concatenate(
        [front_half * cosine - back_half * sine_part, back_half * cosine + front_half * sine_part],
        axis=-1,
    )


def project(token_rows, attn_gain, w_query, key_weight, value_weight, positions):
    normalized_rows = rms_scale(token_rows.astype(jnp.float32), attn_gain).astype(jnp.bfloat16)
    head_size = key_weight.shape[1]
    queries = jnp.dot(normalized_rows, w_query, preferred_element_type=jnp.float32).reshape(
        token_rows.shape[0], -1, head_size
    )
    fresh_key = jnp.dot(normalized_rows, key_weight, preferred_element_type=jnp.float32)
    fresh_value = jnp.dot(normalized_rows, value_weight, preferred_element_type=jnp.float32).astype(
        jnp.bfloat16
    )
    queries = rotate(rms_scale(queries, 1.0), positions[:, None]).astype(jnp.bfloat16)
    fresh_key = rotate(rms_scale(fresh_key, 1.0), positions).astype(jnp.bfloat16)
    return (queries, fresh_key, fresh_value)


def pool_pages(page_table, lengths_here, pool_size, page_len):
    requests_here, max_pages = page_table.shape
    counts = (lengths_here + page_len - 1) // page_len
    matched = (page_table[:, :, None] == jnp.arange(pool_size)[None, None, :]) & (
        jnp.arange(max_pages)[None, :, None] < counts[:, None, None]
    )
    owned_by = jnp.any(matched, axis=1)
    in_use = jnp.any(owned_by, axis=0)
    owners = jnp.sum(
        owned_by.astype(jnp.int32) * jnp.arange(requests_here, dtype=jnp.int32)[:, None], axis=0
    )
    page_pos = jnp.sum(
        matched.astype(jnp.int32) * jnp.arange(max_pages, dtype=jnp.int32)[None, :, None],
        axis=(0, 1),
    )
    return (owners, page_pos, in_use)


def attend(queries, key_self, value_self, page_sets, lengths_here):
    head_size = queries.shape[-1]
    scale_factor = 1.0 / math.sqrt(head_size)
    requests_here = queries.shape[0]
    self_score = (
        jnp.einsum("rgh,rh->rg", queries, key_self, preferred_element_type=jnp.float32)
        * scale_factor
    )
    best_score = self_score
    prepared = []
    for page_keys, page_values, owners, page_pos, in_use in page_sets:
        page_len = page_keys.shape[1]
        member = (owners[:, None] == jnp.arange(requests_here)[None, :]) & in_use[:, None]
        page_queries = jnp.take(queries, owners, axis=0)
        scores = (
            jnp.einsum("pgh,pth->pgt", page_queries, page_keys, preferred_element_type=jnp.float32)
            * scale_factor
        )
        position = page_pos[:, None] * page_len + jnp.arange(page_len)[None, :]
        usable = (position < jnp.take(lengths_here, owners)[:, None]) & in_use[:, None]
        page_best = jnp.max(jnp.where(usable[:, None, :], scores, -jnp.inf), axis=2)
        best_score = jnp.maximum(
            best_score,
            jnp.max(jnp.where(member[:, :, None], page_best[:, None, :], -jnp.inf), axis=0),
        )
        prepared.append((scores, usable, member, owners, page_values))
    self_weight = jnp.exp(self_score - best_score)
    rounded_self = lax.optimization_barrier(self_weight.astype(jnp.bfloat16)).astype(jnp.float32)
    denominator = self_weight
    summed = rounded_self[:, :, None] * value_self.astype(jnp.float32)[:, None, :]
    for scores, usable, member, owners, page_values in prepared:
        shifted = scores - jnp.take(best_score, owners, axis=0)[:, :, None]
        weights = jnp.where(usable[:, None, :], jnp.exp(jnp.minimum(shifted, 0.0)), 0.0)
        selector = member.astype(jnp.float32)
        denominator = denominator + jnp.dot(
            selector.T, jnp.sum(weights, axis=2), precision=lax.Precision.HIGHEST
        )
        page_out = jnp.einsum(
            "pgt,pth->pgh",
            weights.astype(jnp.bfloat16),
            page_values,
            preferred_element_type=jnp.float32,
        )
        summed = summed + jnp.dot(
            selector.T, page_out.reshape(page_out.shape[0], -1), precision=lax.Precision.HIGHEST
        ).reshape(summed.shape)
    return (summed / denominator[:, :, None]).reshape(requests_here, -1).astype(jnp.bfloat16)


def body(
    tokens,
    lengths,
    page_table,
    key_cache,
    value_page_cache,
    mig_slot,
    attn_gain,
    w_query,
    key_weight,
    value_weight,
    w_out,
    moe_gain,
    routes,
    gate_probs,
    w_gate,
    w_up,
    w_down,
):
    req_count = lax.axis_size("req")
    kv_count = lax.axis_size("kv")
    req_here = lax.axis_index("req")
    kv_here = lax.axis_index("kv")
    requests_here, model_width = tokens.shape
    pool_size = key_cache.shape[0]
    page_len = key_cache.shape[2]
    max_pages = page_table.shape[1]
    migrants = mig_slot.shape[1]
    max_len = max_pages * page_len
    partner = (req_here + req_count // 2) % req_count
    own_lengths = lax.dynamic_slice_in_dim(lengths, req_here * requests_here, requests_here)
    own_slots = lax.dynamic_index_in_dim(mig_slot, req_here, 0, keepdims=False)
    partner_slots = lax.dynamic_index_in_dim(mig_slot, partner, 0, keepdims=False)
    partner_lengths = jnp.take(
        lax.dynamic_slice_in_dim(lengths, partner * requests_here, requests_here), partner_slots
    )
    post_lengths = own_lengths.at[own_slots].set(partner_lengths)
    pool_keys = key_cache[:, 0]
    pool_values = value_page_cache[:, 0]
    owners, page_pos, in_use = pool_pages(page_table, own_lengths, pool_size, page_len)
    depart_pages = jnp.take(page_table, own_slots, axis=0)
    depart_mask = jnp.arange(max_len)[None, :] < jnp.take(own_lengths, own_slots)[:, None]
    depart_keys = jnp.where(
        depart_mask[:, :, None],
        jnp.take(pool_keys, depart_pages, axis=0).reshape(migrants, max_len, -1),
        jnp.zeros((), jnp.bfloat16),
    )
    depart_values = jnp.where(
        depart_mask[:, :, None],
        jnp.take(pool_values, depart_pages, axis=0).reshape(migrants, max_len, -1),
        jnp.zeros((), jnp.bfloat16),
    )
    leaving_tokens = jnp.take(tokens, own_slots, axis=0)
    arrived_keys, arrived_values, arrived_tokens = from_behind(
        (depart_keys, depart_values, leaving_tokens), "req", req_count // 2
    )
    settled_tokens = tokens.at[own_slots].set(arrived_tokens)
    queries, fresh_key, fresh_value = project(
        settled_tokens, attn_gain, w_query, key_weight, value_weight, post_lengths
    )
    staying = in_use & jnp.logical_not(jnp.any(owners[:, None] == own_slots[None, :], axis=1))
    arrival_set = (
        arrived_keys.reshape(migrants * max_pages, page_len, -1),
        arrived_values.reshape(migrants * max_pages, page_len, -1),
        jnp.repeat(own_slots, max_pages),
        jnp.tile(jnp.arange(max_pages, dtype=jnp.int32), migrants),
        jnp.ones((migrants * max_pages,), jnp.bool_),
    )
    attended = attend(
        queries,
        fresh_key,
        fresh_value,
        [(pool_keys, pool_values, owners, page_pos, staying), arrival_set],
        post_lengths,
    )
    disp_rows = requests_here // kv_count
    totals = lax.psum(
        jnp.dot(attended, w_out, preferred_element_type=jnp.float32).astype(jnp.bfloat16), "kv"
    ).astype(jnp.float32)
    projected = lax.dynamic_slice_in_dim(totals, kv_here * disp_rows, disp_rows)
    residual_rows = lax.dynamic_slice_in_dim(settled_tokens, kv_here * disp_rows, disp_rows).astype(
        jnp.float32
    )
    hidden = (residual_rows + projected).astype(jnp.bfloat16)
    moe_in = rms_scale(hidden.astype(jnp.float32), moe_gain).astype(jnp.bfloat16)
    devices = req_count * kv_count
    local_experts = w_gate.shape[0]
    expert_total = devices * local_experts
    top_count = routes.shape[1]
    capacity = max(2, 2 * disp_rows * top_count // expert_total)
    flat_routes = routes.reshape(-1)
    expert_hot = (
        flat_routes[:, None] == jnp.arange(expert_total, dtype=jnp.int32)[None, :]
    ).astype(jnp.int32)
    ranking = jnp.sum((jnp.cumsum(expert_hot, axis=0) - expert_hot) * expert_hot, axis=1)
    slot_index = flat_routes * capacity + ranking
    placement = (
        jnp.arange(expert_total * capacity, dtype=jnp.int32)[:, None] == slot_index[None, :]
    ).reshape(expert_total * capacity, disp_rows, top_count)
    placement = jnp.any(placement, axis=2).astype(jnp.bfloat16)
    outgoing = jnp.dot(placement, moe_in, preferred_element_type=jnp.float32).astype(jnp.bfloat16)
    outgoing = outgoing.reshape(devices, local_experts, capacity, model_width)
    received = lax.all_to_all(outgoing, ("req", "kv"), split_axis=0, concat_axis=0, tiled=True)
    gate_part = jnp.einsum("sexd,edf->sexf", received, w_gate, preferred_element_type=jnp.float32)
    up_part = jnp.einsum("sexd,edf->sexf", received, w_up, preferred_element_type=jnp.float32)
    activated = (jax.nn.silu(gate_part) * up_part).astype(jnp.bfloat16)
    returned = lax.all_to_all(
        jnp.einsum("sexf,efd->sexd", activated, w_down, preferred_element_type=jnp.float32).astype(
            jnp.bfloat16
        ),
        ("req", "kv"),
        split_axis=0,
        concat_axis=0,
        tiled=True,
    )
    picked = jnp.take(returned.reshape(-1, model_width), slot_index, axis=0).reshape(
        disp_rows, top_count, model_width
    )
    shares = gate_probs / jnp.sum(gate_probs, axis=1, keepdims=True)
    mixed_rows = hidden.astype(jnp.float32) + jnp.sum(
        shares[:, :, None] * picked.astype(jnp.float32), axis=1
    )
    return (mixed_rows.astype(jnp.bfloat16), arrived_keys[:, None], arrived_values[:, None])


def solution(mesh):
    in_specs = (
        P("req", None),
        P(),
        P("req", None),
        P("req", "kv", None, None),
        P("req", "kv", None, None),
        P(),
        P(),
        P(None, "kv"),
        P(None, "kv"),
        P(None, "kv"),
        P("kv", None),
        P(),
        P(("req", "kv"), None),
        P(("req", "kv"), None),
        P(("req", "kv"), None, None),
        P(("req", "kv"), None, None),
        P(("req", "kv"), None, None),
    )
    out_specs = (P(("req", "kv"), None), P("req", "kv", None, None), P("req", "kv", None, None))
    return jax.shard_map(body, mesh=mesh, in_specs=in_specs, out_specs=out_specs, check_vma=False)
```

profile of v0, /device:TPU:1, one launch (start us, length us, event | category | flops | bytes accessed | tf_op | source)
XLA Modules:
  0.0 262.2 jit_solution(586046590555309745)
XLA Ops:
  7.2 2.0 copy.167
  9.3 1.0 dynamic-slice_reduce_fusion
  10.3 0.8 and_select_fusion.1
  11.1 0.6 gather_fusion.10
  11.7 1.7 gather_fusion
  13.5 3.8 %collective-permute-start = (bf16[2,2048]{1,0:T(2,128)(2,1)S(1)}, bf16[2,2048]{1,0:T(2,128)(2,1)S(1)}, u32[]{:S(2)}, u32[]{:S(2)}) collective-permute-start(bf16[2,2048]{1,0:T(2,128)(2,1)S(1)} %broadcast_select_fusion.3), channel_id=1, source_target_pairs={{0,64},{4,68},{8,72},{12,76},{16,80},{20,84},{24,88},{28,92},{32,9... | collective-permute-start | bytes 24584 | tf_op jit(solution)/shard_map/ppermute | solution.py:14
  17.3 0.8 copy.105
  18.1 0.6 gather_fusion.5
  18.8 4.1 %gather_fusion.12 = bf16[32,64,128]{2,1,0:T(8,128)(2,1)} fusion(bf16[368,64,128]{2,1,0:T(8,128)(2,1)} %bitcast.173, s32[1024]{0:T(1024)S(1)} %pad_clamp_fusion.1), kind=kCustom, calls=%fused_computation.3.clone | custom fusion | bytes 1048704 | tf_op jit(solution)/shard_map/jit(_take)/gather | solution.py:168
  22.9 4.1 %gather_fusion.11 = bf16[32,64,128]{2,1,0:T(8,128)(2,1)} fusion(bf16[368,64,128]{2,1,0:T(8,128)(2,1)} %bitcast.172, s32[1024]{0:T(1024)S(1)} %pad_clamp_fusion.1), kind=kCustom, calls=%fused_computation.1.clone | custom fusion | bytes 1048704 | tf_op jit(solution)/shard_map/jit(_take)/gather | solution.py:163
  27.1 1.4 broadcast_select_fusion
  28.5 1.3 bitcast_select_fusion.1
  29.9 3.0 %collective-permute-start.2 = (bf16[2,1024,128]{2,1,0:T(8,128)(2,1)}, bf16[2,1024,128]{2,1,0:T(8,128)(2,1)}, u32[]{:S(2)}, u32[]{:S(2)}) collective-permute-start(bf16[2,1024,128]{2,1,0:T(8,128)(2,1)} %get-tuple-element.32), channel_id=1, source_target_pairs={{0,64},{4,68},{8,72},{12,76},{16,80},{20,84},{24,88},{28,92},{32,9... | collective-permute-start | bytes 1572872 | tf_op jit(solution)/shard_map/ppermute | solution.py:14
  33.6 0.7 select_reduce_fusion
  34.5 0.6 gather_fusion.9
  35.1 0.6 scatter_fusion.1
  35.8 2.7 %gather_fusion.1 = s32[368]{0:T(512)S(1)} fusion(s32[128]{0:T(128)S(1)} %scatter_fusion.1, s32[1024]{0:T(1024)S(1)} %pad_clamp_fusion.4), kind=kCustom, calls=%fused_computation.5 | custom fusion | bytes 4416 | tf_op jit(solution)/shard_map/jit(_take)/gather | solution.py:89
  39.0 0.8 fusion.64
  39.8 0.7 gather_fusion.3
  40.5 0.7 iota_compare_fusion.4
  42.3 0.6 copy-done.7
  43.3 2.5 scatter_fusion
  45.8 1.2 fusion.47
  47.1 3.1 %convolution_bitcast_fusion = f32[16,8,8,128]{3,1,2,0:T(8,128)S(1)} fusion(bf16[2048,1024]{1,0:T(8,128)(2,1)} %param.28, bf16[128,2048]{1,0:T(8,128)(2,1)} %scatter_fusion, f32[2048]{0:T(1024)S(1)} %copy-done.19, f32[128]{0:T(128)S(1)} %add_rsqrt_fusion.3), kind=kOutput, calls=%fused_computation.55 | convolution fusion | flops 537919488 | bytes 5251584 | tf_op jit(solution)/shard_map/dot_general | solution.py:40
  50.3 0.8 copy-done.2
  51.5 2.0 broadcast_multiply_fusion
  53.6 1.6 multiply_reduce_fusion.3
  55.7 1.4 subtract_convert_fusion
  57.2 0.9 multiply_reduce_fusion.1
  58.1 2.5 gather_fusion.2
  60.6 0.7 gather_fusion.4
  61.3 0.9 copy.124
  62.2 1.6 fusion.42
  63.8 0.7 copy.106
  64.5 7.4 %select_reduce_fusion.2 = (f32[368,8]{1,0:T(8,128)S(1)}, f32[368,8,64]{2,1,0:T(8,128)}) fusion(pred[368,64]{1,0:T(8,128)(4,1)S(1)} %fusion.65, bf16[368,1,64,128]{3,2,1,0:T(8,128)(2,1)} %param.24, bf16[368,8,128]{2,1,0:T(8,128)(2,1)} %gather_fusion.2, pred[368]{0:T(512)(128)(4,1)} %get-tuple-element.18), kind=kOutput, calls=%fused_computation.48 | convolution fusion | flops 49173632 | bytes 7572336 | tf_op jit(solution)/shard_map/pgh,pth->pgt/dot_general | solution.py:85
  72.4 1.6 select_reduce_fusion.5
  74.1 0.6 fusion.91
  75.3 1.3 gather_fusion.7
  76.6 1.2 gather_fusion.6
  77.9 0.9 broadcast_select_fusion.4
  78.8 0.7 broadcast_select_fusion.2
  79.5 2.3 fusion.40
  82.1 3.8 %fusion.51 = f32[368,8,128]{2,1,0:T(8,128)S(1)} fusion(f32[368,8,64]{2,1,0:T(8,128)S(1)} %copy-done.1, f32[368,8]{1,0:T(8,128)S(1)} %broadcast_select_fusion.2, pred[368,64]{1,0:T(8,128)(4,1)S(1)} %copy-done.6, bf16[368,1,64,128]{3,2,1,0:T(8,128)(2,1)} %param.25), kind=kOutput, calls=%fused_computation.70 | convolution fusion | flops 48988160 | bytes 8325632 | tf_op jit(solution)/shard_map/pgt,pth->pgh/dot_general | solution.py:107
  85.9 1.3 fusion.78
  88.0 1.6 fusion.35
  89.5 0.6 fusion.39
  90.2 1.5 convolution_convert_fusion.1
  92.5 41.7 %all-reduce.2.cloned.1.call-done = bf16[128,2048]{1,0:T(8,128)(2,1)} async-done(((bf16[128,2048]{1,0:T(8,128)(2,1)}), bf16[128,2048]{1,0:T(8,128)(2,1)}) %all-reduce.2.cloned.1.call-update) | async-done | bytes 524304 | tf_op jit(solution)/shard_map/psum | solution.py:195
  134.2 1.1 fusion.60
  135.3 2.1 convolution_convert_fusion
  137.4 4.1 %reshape.604 = bf16[128,1,4,2048]{3,2,0,1:T(4,128)(2,1)} reshape(bf16[512,2048]{1,0:T(8,128)(2,1)} %convolution_convert_fusion) | data formatting | bytes 4194304 | tf_op jit(solution)/shard_map/reshape | solution.py:220
  141.6 41.6 %all_to_all.10 = bf16[128,1,4,2048]{3,2,1,0:T(4,128)(2,1)S(1)} all-to-all(bf16[128,1,4,2048]{3,2,1,0:T(4,128)(2,1)} %bitcast.171), channel_id=1, replica_groups=mesh['req'=32,'kv'=4] {'req','kv'}, dimensions={0} | all-to-all | bytes 4194304 | tf_op jit(solution)/shard_map/all_to_all | solution.py:221
  183.2 1.3 copy-done.4
  184.5 4.8 %fusion.4 = f32[128,4,768]{2,0,1:T(8,128)} fusion(bf16[1,2048,768]{2,1,0:T(8,128)(2,1)S(1)} %copy-done.32, bf16[128,1,4,2048]{3,2,1,0:T(4,128)(2,1)S(1)} %all_to_all.10), kind=kOutput, calls=%fused_computation.19 | convolution fusion | flops 1610612736 | bytes 6815744 | tf_op jit(solution)/shard_map/sexd,edf->sexf/dot_general | solution.py:222
  189.3 9.9 %fusion.12 = bf16[128,1,4,2048]{3,0,2,1:T(8,128)(2,1)} fusion(bf16[1,768,2048]{2,1,0:T(8,128)(2,1)S(1)} %copy-done, bf16[1,2048,768]{2,1,0:T(8,128)(2,1)} %param.36, bf16[128,1,4,2048]{3,2,1,0:T(4,128)(2,1)} %copy-done.4, f32[128,4,768]{2,0,1:T(8,128)} %fusion.4), kind=kOutput, calls=%fused_computation.28 | convolution fusion | flops 3224633344 | bytes 12058624 | tf_op jit(solution)/shard_map/sexf,efd->sexd/dot_general | solution.py:226
  199.1 4.5 %copy.119 = bf16[128,1,4,2048]{3,2,1,0:T(4,128)(2,1)} copy(bf16[128,1,4,2048]{3,0,2,1:T(8,128)(2,1)} %fusion.12) | data formatting | bytes 4194304 | tf_op jit(solution)/shard_map/convert_element_type | solution.py:226
  203.6 5.1 %all-to-all-start.1 = ((bf16[128,1,4,2048]{3,2,1,0:T(4,128)(2,1)}), bf16[128,1,4,2048]{3,2,1,0:T(4,128)(2,1)}, u32[]{:S(2)}, u32[]{:S(2)}) async-start(bf16[128,1,4,2048]{3,2,1,0:T(4,128)(2,1)} %copy.119), calls=%async_computation.1 | async-start | bytes 4194304 | tf_op jit(solution)/shard_map/all_to_all | solution.py:225
  209.0 29.8 %all-to-all-done.1 = bf16[128,1,4,2048]{3,2,1,0:T(4,128)(2,1)} async-done(((bf16[128,1,4,2048]{3,2,1,0:T(4,128)(2,1)}), bf16[128,1,4,2048]{3,2,1,0:T(4,128)(2,1)}, u32[]{:S(2)}, u32[]{:S(2)}) %all-to-all-start.1) | async-done | bytes 2097184 | tf_op jit(solution)/shard_map/all_to_all | solution.py:225
  238.8 4.0 %reshape.610 = bf16[512,2048]{1,0:T(8,128)(2,1)} reshape(bf16[128,1,4,2048]{3,2,1,0:T(4,128)(2,1)} %all-to-all-done.1) | data formatting | bytes 4194304 | tf_op jit(solution)/shard_map/reshape | solution.py:234
  242.8 5.2 %gather_fusion.8 = bf16[256,2048]{1,0:T(8,128)(2,1)} fusion(bf16[512,2048]{1,0:T(8,128)(2,1)} %reshape.610, s32[1024]{0:T(1024)S(1)} %pad_clamp_fusion), kind=kCustom, calls=%fused_computation.12 | custom fusion | bytes 2098176 | tf_op jit(solution)/shard_map/jit(_take)/gather | solution.py:234
  248.0 2.9 %multiply_reduce_fusion = f32[32,2048]{1,0:T(8,128)S(1)} fusion(bf16[256,2048]{1,0:T(8,128)(2,1)} %gather_fusion.8, f32[32,8]{1,0:T(8,128)S(1)} %copy.111, pred[32,8]{1,0:T(8,128)(4,1)S(1)} %get-tuple-element.9), kind=kLoop, calls=%fused_computation.32 | loop fusion | flops 2031616 | bytes 1312000 | tf_op jit(solution)/shard_map/reduce_sum | solution.py:238
  250.9 0.7 fusion.63
  251.6 1.9 copy.168
  253.5 1.9 copy.169
  (146 shorter events, 7.4 us)
Async XLA Ops:
  7.2 182.1 %copy-start = (bf16[1,768,2048]{2,1,0:T(8,128)(2,1)S(1)}, bf16[1,768,2048]{2,1,0:T(8,128)(2,1)}, u32[]{:S(2)}) copy-start(bf16[1,768,2048]{2,1,0:T(8,128)(2,1)} %param.37) | copy-start | bytes 9437188
  7.2 127.0 %all-reduce.2.cloned.1.call-start = ((), (), s32[]{:S(2)}) async-start(), calls=%async_computation.2 | async-start | bytes 1048576 | tf_op jit(solution)/shard_map/psum | solution.py:195
  13.5 29.8 %collective-permute-start = (bf16[2,2048]{1,0:T(2,128)(2,1)S(1)}, bf16[2,2048]{1,0:T(2,128)(2,1)S(1)}, u32[]{:S(2)}, u32[]{:S(2)}) collective-permute-start(bf16[2,2048]{1,0:T(2,128)(2,1)S(1)} %broadcast_select_fusion.3), channel_id=1, source_target_pairs={{0,64},{4,68},{8,72},{12,76},{16,80},{20,84},{24,88},{28,92},{32,9... | collective-permute-start | bytes 24584 | tf_op jit(solution)/shard_map/ppermute | solution.py:14
  27.1 5.7 %copy-start.11 = (s32[128,16]{0,1:T(8,128)S(1)}, s32[128,16]{0,1:T(8,128)}, u32[]{:S(2)}) copy-start(s32[128,16]{0,1:T(8,128)} %param.23) | copy-start | bytes 24580
  29.8 42.6 %collective-permute-start.1 = (bf16[2,1024,128]{2,1,0:T(8,128)(2,1)}, bf16[2,1024,128]{2,1,0:T(8,128)(2,1)}, u32[]{:S(2)}, u32[]{:S(2)}) collective-permute-start(bf16[2,1024,128]{2,1,0:T(8,128)(2,1)} %get-tuple-element.33), channel_id=1, source_target_pairs={{0,64},{4,68},{8,72},{12,76},{16,80},{20,84},{24,88},{28,92},{32,9... | collective-permute-start | bytes 1572872 | tf_op jit(solution)/shard_map/ppermute | solution.py:14
  29.9 56.1 %collective-permute-start.2 = (bf16[2,1024,128]{2,1,0:T(8,128)(2,1)}, bf16[2,1024,128]{2,1,0:T(8,128)(2,1)}, u32[]{:S(2)}, u32[]{:S(2)}) collective-permute-start(bf16[2,1024,128]{2,1,0:T(8,128)(2,1)} %get-tuple-element.32), channel_id=1, source_target_pairs={{0,64},{4,68},{8,72},{12,76},{16,80},{20,84},{24,88},{28,92},{32,9... | collective-permute-start | bytes 1572872 | tf_op jit(solution)/shard_map/ppermute | solution.py:14
  34.5 6.7 %copy-start.28 = (s32[32]{0:T(128)}, s32[32]{0:T(128)S(1)}, u32[]{:S(2)}) copy-start(s32[32]{0:T(128)S(1)} %eq.110) | copy-start | bytes 388
  34.5 7.3 %copy-start.27 = (s32[32,8]{0,1:T(8,128)S(1)}, s32[32,8]{0,1:T(8,128)}, u32[]{:S(2)}) copy-start(s32[32,8]{0,1:T(8,128)} %param.33) | copy-start | bytes 3076
  35.7 11.3 %copy-start.19 = (f32[2048]{0:T(1024)S(1)}, f32[2048]{0:T(1024)}, u32[]{:S(2)}) copy-start(f32[2048]{0:T(1024)} %param.27) | copy-start | bytes 24580
  35.8 22.4 %copy-start.12 = (s32[1024]{0:T(1024)}, s32[1024]{0:T(1024)S(1)}, u32[]{:S(2)}) copy-start(s32[1024]{0:T(1024)S(1)} %pad_clamp_fusion.4) | copy-start | bytes 12292
  39.0 11.2 %copy-start.25 = (pred[368]{0:T(512)(128)(4,1)}, pred[368]{0:T(512)(128)(4,1)S(1)}, u32[]{:S(2)}) copy-start(pred[368]{0:T(512)(128)(4,1)S(1)} %not_and_fusion) | copy-start | bytes 1108
  39.8 1.9 copy-start.22
  42.3 0.7 copy-start.7
  43.2 21.4 %copy-start.5 = (pred[368,64]{1,0:T(8,128)(4,1)}, pred[368,64]{1,0:T(8,128)(4,1)S(1)}, u32[]{:S(2)}) copy-start(pred[368,64]{1,0:T(8,128)(4,1)S(1)} %fusion.65) | copy-start | bytes 70660
  43.3 6.9 %copy-start.24 = (s32[128,3]{0,1:T(4,128)}, s32[128,3]{0,1:T(4,128)S(1)}, u32[]{:S(2)}) copy-start(s32[128,3]{0,1:T(4,128)S(1)} %reduce-window.9) | copy-start | bytes 4612
  47.1 6.5 %copy-start.30 = (f32[128]{0:T(128)}, f32[128]{0:T(128)S(1)}, u32[]{:S(2)}) copy-start(f32[128]{0:T(128)S(1)} %add_rsqrt_fusion.3) | copy-start | bytes 1540
  50.3 0.8 copy-start.2
  55.7 6.5 %copy-start.31 = (f32[128]{0:T(128)S(1)}, f32[128]{0:T(128)}, u32[]{:S(2)}) copy-start(f32[128]{0:T(128)} %copy-done.30) | copy-start | bytes 1540
  62.2 11.9 %copy-start.14 = (f32[128,8]{0,1:T(8,128)}, f32[128,8]{0,1:T(8,128)S(1)}, u32[]{:S(2)}) copy-start(f32[128,8]{0,1:T(8,128)S(1)} %copy.124) | copy-start | bytes 12292
  64.5 7.4 %copy-start.10 = (pred[368,128]{1,0:T(8,128)(4,1)S(1)}, pred[368,128]{1,0:T(8,128)(4,1)}, u32[]{:S(2)}) copy-start(pred[368,128]{1,0:T(8,128)(4,1)} %fusion.64) | copy-start | bytes 141316
  64.5 7.9 %copy-start.23 = (pred[32]{0:T(512)(128)(4,1)S(1)}, pred[32]{0:T(512)(128)(4,1)}, u32[]{:S(2)}) copy-start(pred[32]{0:T(512)(128)(4,1)} %get-tuple-element.20) | copy-start | bytes 100
  64.5 9.5 %copy-start.18 = (pred[32,128]{1,0:T(8,128)(4,1)S(1)}, pred[32,128]{1,0:T(8,128)(4,1)}, u32[]{:S(2)}) copy-start(pred[32,128]{1,0:T(8,128)(4,1)} %iota_compare_fusion.4) | copy-start | bytes 12292
  74.7 0.6 copy-start.16
  77.8 4.2 %copy-start.1 = (f32[368,8,64]{2,1,0:T(8,128)S(1)}, f32[368,8,64]{2,1,0:T(8,128)}, u32[]{:S(2)}) copy-start(f32[368,8,64]{2,1,0:T(8,128)} %get-tuple-element.45) | copy-start | bytes 2260996
  77.9 4.2 %copy-start.6 = (pred[368,64]{1,0:T(8,128)(4,1)S(1)}, pred[368,64]{1,0:T(8,128)(4,1)}, u32[]{:S(2)}) copy-start(pred[368,64]{1,0:T(8,128)(4,1)} %copy-done.5) | copy-start | bytes 70660
  82.0 5.3 %copy-start.15 = (f32[128,8]{0,1:T(8,128)S(1)}, f32[128,8]{0,1:T(8,128)}, u32[]{:S(2)}) copy-start(f32[128,8]{0,1:T(8,128)} %copy-done.14) | copy-start | bytes 12292
  82.0 5.3 %copy-start.17 = (f32[128,8]{0,1:T(8,128)S(1)}, f32[128,8]{0,1:T(8,128)}, u32[]{:S(2)}) copy-start(f32[128,8]{0,1:T(8,128)} %copy-done.16) | copy-start | bytes 12292
  82.0 5.3 %copy-start.26 = (pred[368]{0:T(512)(128)(4,1)S(1)}, pred[368]{0:T(512)(128)(4,1)}, u32[]{:S(2)}) copy-start(pred[368]{0:T(512)(128)(4,1)} %copy-done.25) | copy-start | bytes 1108
  82.1 5.7 %copy-start.21 = (bf16[128,8]{0,1:T(8,128)(2,1)S(1)}, bf16[128,8]{0,1:T(8,128)(2,1)}, u32[]{:S(2)}) copy-start(bf16[128,8]{0,1:T(8,128)(2,1)} %get-tuple-element.13) | copy-start | bytes 6148
  82.1 5.7 %copy-start.29 = (s32[32]{0:T(128)S(1)}, s32[32]{0:T(128)}, u32[]{:S(2)}) copy-start(s32[32]{0:T(128)} %copy-done.28) | copy-start | bytes 388
  82.1 5.9 %copy-start.9 = (f32[128,128]{0,1:T(8,128)S(1)}, f32[128,128]{0,1:T(8,128)}, u32[]{:S(2)}) copy-start(f32[128,128]{0,1:T(8,128)} %copy.106) | copy-start | bytes 196612
  87.8 2.4 copy-start.3
  90.2 1.6 slice-start
  90.2 1.6 copy-start.8
  90.2 45.1 %copy-start.20 = (f32[2048]{0:T(1024)S(1)}, f32[2048]{0:T(1024)}, u32[]{:S(2)}) copy-start(f32[2048]{0:T(1024)} %param.32) | copy-start | bytes 24580
  141.6 42.9 %copy-start.32 = (bf16[1,2048,768]{2,1,0:T(8,128)(2,1)S(1)}, bf16[1,2048,768]{2,1,0:T(8,128)(2,1)}, u32[]{:S(2)}) copy-start(bf16[1,2048,768]{2,1,0:T(8,128)(2,1)} %param.35) | copy-start | bytes 9437188
  183.2 1.3 copy-start.4
  203.6 5.2 %copy-start.13 = (f32[32,8]{0,1:T(8,128)S(1)}, f32[32,8]{0,1:T(8,128)}, u32[]{:S(2)}) copy-start(f32[32,8]{0,1:T(8,128)} %param.34) | copy-start | bytes 3076
  203.6 35.2 %all-to-all-start.1 = ((bf16[128,1,4,2048]{3,2,1,0:T(4,128)(2,1)}), bf16[128,1,4,2048]{3,2,1,0:T(4,128)(2,1)}, u32[]{:S(2)}, u32[]{:S(2)}) async-start(bf16[128,1,4,2048]{3,2,1,0:T(4,128)(2,1)} %copy.119), calls=%async_computation.1 | async-start | bytes 4194304 | tf_op jit(solution)/shard_map/all_to_all | solution.py:225
Sparse Core Ops, SparseCore 0:
  91.9 42.2 all-reduce.1
where the time goes:
time: 263 us; the launch traced here: 262 us
  waiting for transfers between devices  71.6 us (27%)
  local copies, waits for them, and re-layouts  55.9 us (21%)
  matrix products  41.6 us (16%)
  blocking collectives  41.6 us (16%)
  other arithmetic  24.9 us (9%)
  between operations  14.7 us (6%)
  starting transfers between devices  11.9 us (5%)
    psum x1, waiting for transfers between devices, body(): lax.psum(jnp.dot(attended, w_out, preferred_element_type=jnp.float32).ast...  41.7 us
    all_to_all x1, blocking collectives, body(): lax.all_to_all(outgoing, ('req', 'kv'), split_axis=0, concat_axis=0, tile...  41.6 us
    all_to_all x1, waiting for transfers between devices, body(): lax.all_to_all(jnp.einsum('sexf,efd->sexd', activated, w_down, preferred_...  29.8 us
    unnamed x74, local copies, waits for them, and re-layouts  10.2 us
    dot_general x1, matrix products, body(): jnp.einsum('sexf,efd->sexd', activated, w_down, preferred_element_type=jn...  9.86 us
    dot_general x2, matrix products, attend(): jnp.einsum('pgh,pth->pgt', page_queries, page_keys, preferred_element_typ...  8.98 us
    ppermute x3, starting transfers between devices, from_behind(): lax.ppermute(shard, axis, [(i, (i + by) % size) for i in range(size)])  6.78 us
  transfers between devices with their start and end apart: 5, of which 2 were waited for; matrix products, arithmetic and copies ran while one was open for 24% of the time, Pallas kernels for 0%

commit v1 on v0

v1 whole, which is shorter than its diff:
```python
import math

import jax
import jax.numpy as jnp
from jax import lax
from jax.experimental import pallas as pl
from jax.experimental.pallas import tpu as pltpu
from jax.sharding import PartitionSpec as P

EPSILON = 1e-06
THETA = 1000000.0
MASKED = -1e30
BF16 = jnp.bfloat16
F32 = jnp.float32
POOL_CUTS = 4
QUERY_CUTS = 4
GROUP = 4
UNROLL_SHORT = 4
UNROLL_LONG = 2


def dot_t(a, b):
    return lax.dot_general(a, b, (((1,), (1,)), ((), ())), preferred_element_type=F32)


def dot_n(a, b):
    return jnp.dot(a, b, preferred_element_type=F32)


def attention_kernel(
    table,
    lens,
    slots,
    tokens,
    gain,
    cos_ref,
    sin_ref,
    wq_hbm,
    wk_hbm,
    wv_hbm,
    k_hbm,
    v_hbm,
    att_out,
    mig_out,
    dk_out,
    dv_out,
    wq,
    wk,
    wv,
    kp,
    vp,
    qs,
    ks,
    vs,
    os,
    mig,
    longs,
    wsem,
    psem,
):
    rows, width = tokens.shape
    pool, page, head = kp.shape
    max_pages = table.shape[1]
    heads = wq.shape[1] // head
    scale = 1.0 / math.sqrt(head)
    wcut = wq.shape[1] // QUERY_CUTS
    pcut = pool // POOL_CUTS

    wcopies = [
        pltpu.make_async_copy(
            wq_hbm.at[:, pl.ds(c * wcut, wcut)], wq.at[:, pl.ds(c * wcut, wcut)], wsem.at[c]
        )
        for c in range(QUERY_CUTS)
    ]
    wcopies.append(pltpu.make_async_copy(wk_hbm, wk, wsem.at[QUERY_CUTS]))
    wcopies.append(pltpu.make_async_copy(wv_hbm, wv, wsem.at[QUERY_CUTS + 1]))
    pcopies = []
    for i, (src, dst) in enumerate(((k_hbm, kp), (v_hbm, vp))):
        for c in range(POOL_CUTS):
            pcopies.append(
                pltpu.make_async_copy(
                    src.at[pl.ds(c * pcut, pcut), 0],
                    dst.at[pl.ds(c * pcut, pcut)],
                    psem.at[i * POOL_CUTS + c],
                )
            )
    for copy in wcopies + pcopies:
        copy.start()

    def gather_long(r, n):
        is_long = lens[r] > page

        @pl.when(is_long)
        def _():
            longs[n] = r

        return n + is_long.astype(jnp.int32)

    long_count = lax.fori_loop(0, rows, gather_long, jnp.int32(0))

    x = tokens[...].astype(F32)
    row_id = lax.broadcasted_iota(jnp.int32, (rows, 1), 0)
    for k in range(2):
        leaving = jnp.sum(jnp.where(row_id == slots[k], x, 0.0), axis=0, keepdims=True)
        for c in range(width // head):
            mig[k * 24 + 8 + c : k * 24 + 9 + c, :] = leaving[:, c * head : (c + 1) * head]
    normed = (
        x * lax.rsqrt(jnp.mean(x * x, axis=-1, keepdims=True) + EPSILON) * gain[...]
    ).astype(BF16)
    cos = cos_ref[...]
    sin = sin_ref[...]

    def rotated(vectors):
        unit = vectors * lax.rsqrt(jnp.mean(vectors * vectors, axis=-1, keepdims=True) + EPSILON)
        turned = unit * cos + pltpu.roll(unit, head // 2, 1) * sin
        return turned.astype(BF16).astype(F32)

    per_cut = wcut // head
    for c in range(QUERY_CUTS):
        wcopies[c].wait()
        query = dot_n(normed, wq[:, c * wcut : (c + 1) * wcut])
        for i in range(per_cut):
            qs[pl.ds(c * per_cut + i, rows, stride=heads), :] = rotated(
                query[:, i * head : (i + 1) * head]
            )
    wcopies[QUERY_CUTS].wait()
    wcopies[QUERY_CUTS + 1].wait()
    fresh_key = rotated(dot_n(normed, wk[...]))
    fresh_value = dot_n(normed, wv[...]).astype(BF16).astype(F32)
    for h in range(heads):
        ks[pl.ds(h, rows, stride=heads), :] = fresh_key
        vs[pl.ds(h, rows, stride=heads), :] = fresh_value

    for copy in pcopies:
        copy.wait()

    def softmax_out(query, base, count, scores, valid, values):
        scores = jnp.where(valid, scores * scale, MASKED)
        self_score = jnp.sum(query * ks[pl.ds(base, count), :], axis=1, keepdims=True) * scale
        top = jnp.maximum(jnp.max(scores, axis=1, keepdims=True), self_score)
        weights = jnp.exp(scores - top)
        self_weight = jnp.exp(self_score - top)
        total = jnp.sum(weights, axis=1, keepdims=True) + self_weight
        summed = dot_n(weights.astype(BF16), values)
        summed = summed + self_weight.astype(BF16).astype(F32) * vs[pl.ds(base, count), :]
        os[pl.ds(base, count), :] = summed / total

    lanes = lax.broadcasted_iota(jnp.int32, (GROUP * heads, GROUP * page), 1)
    subs = lax.broadcasted_iota(jnp.int32, (GROUP * heads, GROUP * page), 0)
    place = jnp.where(lanes // page == subs // heads, lanes % page, 1 << 20)
    lane_row = lax.broadcasted_iota(jnp.int32, (1, GROUP * page), 1)

    def short_group(g):
        first = g * GROUP
        base = pl.multiple_of(first * heads, GROUP * heads)
        pages = [table[first + i, 0] for i in range(GROUP)]
        keys = jnp.concatenate([kp[p] for p in pages], axis=0)
        values = jnp.concatenate([vp[p] for p in pages], axis=0)
        limit = jnp.full((1, GROUP * page), lens[first], jnp.int32)
        for i in range(1, GROUP):
            limit = jnp.where(lane_row >= i * page, lens[first + i], limit)
        query = qs[pl.ds(base, GROUP * heads), :]
        scores = dot_t(query.astype(BF16), keys)
        softmax_out(query, base, GROUP * heads, scores, place < limit, values)

    def short_step(step, carry):
        for u in range(UNROLL_SHORT):
            short_group(step * UNROLL_SHORT + u)
        return carry

    lax.fori_loop(0, rows // (GROUP * UNROLL_SHORT), short_step, 0)

    span = lax.broadcasted_iota(jnp.int32, (heads, max_pages * page), 1)

    def long_one(r):
        base = pl.multiple_of(r * heads, heads)
        query = qs[pl.ds(base, heads), :]
        query16 = query.astype(BF16)
        pages = [table[r, j] for j in range(max_pages)]
        scores = []
        for c in range(max_pages // 4):
            keys = jnp.concatenate([kp[pages[c * 4 + i]] for i in range(4)], axis=0)
            scores.append(dot_t(query16, keys))
        scores = jnp.concatenate(scores, axis=1)
        values = jnp.concatenate([vp[p] for p in pages], axis=0)
        softmax_out(query, base, heads, scores, span < lens[r], values)

    def long_step(step, carry):
        for u in range(UNROLL_LONG):
            long_one(longs[jnp.minimum(step * UNROLL_LONG + u, long_count - 1)])
        return carry

    lax.fori_loop(0, (long_count + UNROLL_LONG - 1) // UNROLL_LONG, long_step, 0)

    for h in range(heads):
        att_out[:, h * head : (h + 1) * head] = os[pl.ds(h, rows, stride=heads), :].astype(BF16)
    for k in range(2):
        mig[k * 24 : k * 24 + 8, :] = os[pl.ds(pl.multiple_of(slots[k] * heads, heads), heads), :]
    mig_out[...] = mig[...].astype(BF16)

    in_page = lax.broadcasted_iota(jnp.int32, (page, head), 0)
    for k in range(2):

        def depart(j, carry, k=k):
            row = slots[k]
            held = table[row, j]
            keep = in_page < lens[row] - j * page
            at = pl.multiple_of(j * page, page)
            dk_out[k, pl.ds(at, page), :] = jnp.where(keep, kp[held].astype(F32), 0.0).astype(BF16)
            dv_out[k, pl.ds(at, page), :] = jnp.where(keep, vp[held].astype(F32), 0.0).astype(BF16)
            return carry

        lax.fori_loop(0, max_pages, depart, 0)


def attention(table, lens, slots, tokens, gain, cos, sin, wq, wk, wv, kc, vc):
    rows, width = tokens.shape
    pool, _, page, head = kc.shape
    heads = wq.shape[1] // head
    span = table.shape[1] * page
    smem = pl.BlockSpec(memory_space=pltpu.SMEM)
    vmem = pl.BlockSpec(memory_space=pltpu.VMEM)
    anyspace = pl.BlockSpec(memory_space=pl.ANY)
    return pl.pallas_call(
        attention_kernel,
        out_shape=(
            jax.ShapeDtypeStruct((rows, heads * head), BF16),
            jax.ShapeDtypeStruct((48, head), BF16),
            jax.ShapeDtypeStruct((2, span, head), BF16),
            jax.ShapeDtypeStruct((2, span, head), BF16),
        ),
        in_specs=[smem, smem, smem, vmem, vmem, vmem, vmem] + [anyspace] * 5,
        out_specs=(vmem, vmem, vmem, vmem),
        scratch_shapes=[
            pltpu.VMEM(wq.shape, BF16),
            pltpu.VMEM(wk.shape, BF16),
            pltpu.VMEM(wv.shape, BF16),
            pltpu.VMEM((pool, page, head), BF16),
            pltpu.VMEM((pool, page, head), BF16),
            pltpu.VMEM((rows * heads, head), F32),
            pltpu.VMEM((rows * heads, head), F32),
            pltpu.VMEM((rows * heads, head), F32),
            pltpu.VMEM((rows * heads, head), F32),
            pltpu.VMEM((48, head), F32),
            pltpu.SMEM((rows,), jnp.int32),
            pltpu.SemaphoreType.DMA((QUERY_CUTS + 2,)),
            pltpu.SemaphoreType.DMA((2 * POOL_CUTS,)),
        ],
        compiler_params=pltpu.CompilerParams(vmem_limit_bytes=40 << 20),
        name="attention",
    )(table, lens, slots, tokens, gain, cos, sin, wq, wk, wv, kc, vc)


def project_kernel(slots, attended, arrived, w_out, partial):
    rows, _ = attended.shape
    head = arrived.shape[1]
    heads = attended.shape[1] // head
    row_id = lax.broadcasted_iota(jnp.int32, (rows, head), 0)
    got = arrived[...].astype(F32)
    pieces = []
    for h in range(heads):
        piece = attended[:, h * head : (h + 1) * head].astype(F32)
        for k in range(2):
            piece = jnp.where(row_id == slots[k], got[k * 24 + h : k * 24 + h + 1, :], piece)
        pieces.append(piece.astype(BF16))
    settled = jnp.concatenate(pieces, axis=1)
    partial[...] = dot_n(settled, w_out[...]).astype(BF16)


def project(slots, attended, arrived, w_out):
    vmem = pl.BlockSpec(memory_space=pltpu.VMEM)
    return pl.pallas_call(
        project_kernel,
        out_shape=jax.ShapeDtypeStruct((attended.shape[0], w_out.shape[1]), BF16),
        in_specs=[pl.BlockSpec(memory_space=pltpu.SMEM), vmem, vmem, vmem],
        out_specs=vmem,
        compiler_params=pltpu.CompilerParams(vmem_limit_bytes=24 << 20),
        name="project",
    )(slots, attended, arrived, w_out)


def expert_kernel(received, wg, wu, wd, out, xs):
    pairs = received.shape[0] // 16
    half = received.shape[1]
    cut = 256
    low = lax.broadcasted_iota(jnp.int32, (pairs, 8, cut), 1) < 4
    for c in range(half // cut):
        part = received[:, c * cut : (c + 1) * cut].astype(F32).reshape(pairs, 2, 8, cut)
        one, two = part[:, 0], part[:, 1]
        left = jnp.where(low, one, pltpu.roll(two, 4, 1))
        right = jnp.where(low, pltpu.roll(one, 4, 1), two)
        xs[:, c * cut : (c + 1) * cut] = left.reshape(pairs * 8, cut).astype(BF16)
        xs[:, half + c * cut : half + (c + 1) * cut] = right.reshape(pairs * 8, cut).astype(BF16)
    inputs = xs[...]
    gate = dot_n(inputs, wg[0])
    up = dot_n(inputs, wu[0])
    act = (gate / (1.0 + jnp.exp(-gate)) * up).astype(BF16)
    for c in range(half // cut):
        left = dot_n(act, wd[0, :, c * cut : (c + 1) * cut]).reshape(pairs, 8, cut)
        right = dot_n(act, wd[0, :, half + c * cut : half + (c + 1) * cut]).reshape(pairs, 8, cut)
        one = jnp.where(low, left, pltpu.roll(right, 4, 1))
        two = jnp.where(low, pltpu.roll(left, 4, 1), right)
        both = jnp.stack([one, two], axis=1).reshape(pairs * 16, cut)
        out[:, c * cut : (c + 1) * cut] = both.astype(BF16)


def expert(received, wg, wu, wd):
    vmem = pl.BlockSpec(memory_space=pltpu.VMEM)
    rows, half = received.shape
    return pl.pallas_call(
        expert_kernel,
        out_shape=jax.ShapeDtypeStruct((rows, half), BF16),
        in_specs=[vmem] * 4,
        out_specs=vmem,
        scratch_shapes=[pltpu.VMEM((rows // 2, 2 * half), BF16)],
        compiler_params=pltpu.CompilerParams(vmem_limit_bytes=40 << 20),
        name="expert",
    )(received, wg, wu, wd)


def body(
    tokens,
    lengths,
    page_table,
    key_cache,
    value_page_cache,
    mig_slot,
    attn_gain,
    w_query,
    key_weight,
    value_weight,
    w_out,
    moe_gain,
    routes,
    gate_probs,
    w_gate,
    w_up,
    w_down,
):
    req_count = lax.axis_size("req")
    kv_count = lax.axis_size("kv")
    req_here = lax.axis_index("req")
    kv_here = lax.axis_index("kv")
    requests_here, model_width = tokens.shape
    head = key_weight.shape[1]
    half = model_width // 2
    lens = lax.dynamic_slice_in_dim(lengths, req_here * requests_here, requests_here)
    slots = lax.dynamic_index_in_dim(mig_slot, req_here, 0, keepdims=False)
    exponent = jnp.arange(head // 2, dtype=F32) * (-2.0 / head)
    angles = lens.astype(F32)[:, None] * THETA**exponent
    cosine, sine = jnp.cos(angles), jnp.sin(angles)
    attended, leaving, depart_keys, depart_values = attention(
        page_table,
        lens,
        slots,
        tokens,
        attn_gain[None, :],
        jnp.concatenate([cosine, cosine], axis=1),
        jnp.concatenate([-sine, sine], axis=1),
        w_query,
        key_weight,
        value_weight,
        key_cache,
        value_page_cache,
    )
    swap = [(i, (i + req_count // 2) % req_count) for i in range(req_count)]
    arrived = lax.ppermute(leaving, "req", swap)
    arrived_keys = lax.ppermute(depart_keys, "req", swap)
    arrived_values = lax.ppermute(depart_values, "req", swap)
    partial = project(slots, attended, arrived, w_out)

    disp_rows = requests_here // kv_count
    partial = partial.reshape(kv_count, disp_rows, model_width)
    total = lax.dynamic_index_in_dim(partial, kv_here, 0, keepdims=False).astype(F32)
    for s in range(1, kv_count):
        block = lax.dynamic_index_in_dim(partial, (kv_here + s) % kv_count, 0, keepdims=False)
        ring = [(i, (i + s) % kv_count) for i in range(kv_count)]
        total = total + lax.ppermute(block, "kv", ring).astype(F32)
    own = lax.dynamic_slice_in_dim(tokens, kv_here * disp_rows, disp_rows)
    row_ids = kv_here * disp_rows + jnp.arange(disp_rows, dtype=jnp.int32)
    arrived_rows = arrived.reshape(2, 24, head)[:, 8:].reshape(2, model_width)
    for k in range(2):
        own = jnp.where((row_ids == slots[k])[:, None], arrived_rows[k][None, :], own)
    hidden = (own.astype(F32) + total).astype(BF16)
    hidden32 = hidden.astype(F32)
    moe_in = (
        hidden32 * lax.rsqrt(jnp.mean(hidden32 * hidden32, axis=-1, keepdims=True) + EPSILON) * moe_gain
    ).astype(BF16)

    devices = req_count * kv_count
    top_count = routes.shape[1]
    capacity = 2 * disp_rows * top_count // devices
    flat_routes = routes.reshape(-1)
    ids = jnp.arange(disp_rows * top_count, dtype=jnp.int32)
    earlier = (flat_routes[:, None] == flat_routes[None, :]) & (ids[None, :] < ids[:, None])
    ranking = jnp.sum(earlier.astype(jnp.int32), axis=1)
    slot_index = (flat_routes * capacity + ranking).reshape(disp_rows, top_count)
    chunk_rows = 2 * capacity
    places = jnp.arange(devices * chunk_rows, dtype=jnp.int32)
    place_slot = (places // chunk_rows) * capacity + places % capacity
    place_half = (places % chunk_rows) // capacity
    hits = place_slot[None, None, :] == slot_index[:, :, None]
    shares = gate_probs / jnp.sum(gate_probs, axis=1, keepdims=True)
    share_map = jnp.sum(jnp.where(hits, shares[:, :, None], 0.0), axis=1)
    hit_map = jnp.any(hits, axis=1)
    halves = place_half[None, :] == jnp.arange(2, dtype=jnp.int32)[:, None]
    both_hits = (halves[:, None, :] & hit_map[None, :, :]).reshape(2 * disp_rows, -1).astype(BF16)
    both_shares = jnp.where(halves[:, None, :], share_map[None, :, :], 0.0).reshape(2 * disp_rows, -1)
    share_high = both_shares.astype(BF16)
    share_low = (both_shares - share_high.astype(F32)).astype(BF16)
    share_rows = jnp.concatenate([share_high, share_low], axis=0)

    stacked = jnp.concatenate([moe_in[:, :half], moe_in[:, half:]], axis=0)
    outgoing = lax.dot_general(
        both_hits, stacked, (((0,), (0,)), ((), ())), preferred_element_type=F32
    ).astype(BF16)
    outgoing = outgoing.reshape(devices, chunk_rows, half)
    received = lax.all_to_all(outgoing, ("req", "kv"), split_axis=0, concat_axis=0, tiled=True)
    made = expert(received.reshape(devices * chunk_rows, half), w_gate, w_up, w_down)
    returned = lax.all_to_all(
        made.reshape(devices, chunk_rows, half), ("req", "kv"), split_axis=0, concat_axis=0, tiled=True
    )
    mixed = dot_n(share_rows, returned.reshape(devices * chunk_rows, half))
    mixed = mixed[: 2 * disp_rows] + mixed[2 * disp_rows :]
    mixed = jnp.concatenate([mixed[:disp_rows], mixed[disp_rows:]], axis=1)
    layer_out = (hidden32 + mixed).astype(BF16)
    return (layer_out, arrived_keys[:, None], arrived_values[:, None])


def solution(mesh):
    in_specs = (
        P("req", None),
        P(),
        P("req", None),
        P("req", "kv", None, None),
        P("req", "kv", None, None),
        P(),
        P(),
        P(None, "kv"),
        P(None, "kv"),
        P(None, "kv"),
        P("kv", None),
        P(),
        P(("req", "kv"), None),
        P(("req", "kv"), None),
        P(("req", "kv"), None, None),
        P(("req", "kv"), None, None),
        P(("req", "kv"), None, None),
    )
    out_specs = (P(("req", "kv"), None), P("req", "kv", None, None), P("req", "kv", None, None))
    return jax.shard_map(body, mesh=mesh, in_specs=in_specs, out_specs=out_specs, check_vma=False)
```

time: 263 us -> 160 us (0.61)
  matrix products: 41.6 us -> 1.2 us
  local copies, waits for them, and re-layouts: 55.9 us -> 17.2 us
  Pallas kernels: 0 us -> 26.8 us
  waiting for transfers between devices: 71.6 us -> 48.7 us
  other arithmetic: 24.9 us -> 5.54 us
  between operations: 14.7 us -> 0.92 us
  starting transfers between devices: 11.9 us -> 15.8 us
    ppermute x3 -> x6, waiting for transfers between devices: 0.01 us -> 48.7 us  [the longest x1 33.1 us: body(): arrived_keys = lax.ppermute(depart_keys, 'req', swap)]
    psum x1 -> x0, waiting for transfers between devices: 41.7 us -> none  [body(): lax.psum(jnp.dot(attended, w_out, preferred_element_type=jnp.float32).ast...]
    dot_general x15 -> x2, matrix products: 41.6 us -> 1.2 us  [the longest x1 0.76 us: body(): lax.dot_general(both_hits, stacked, (((0,), (0,)), ((), ())), preferred_e...]
    all_to_all x1, waiting for transfers between devices: 29.8 us -> 0.01 us  [body(): lax.all_to_all(made.reshape(devices, chunk_rows, half), ('req', 'kv'), sp...]
    pallas_call x0 -> x3, Pallas kernels: none -> 26.8 us  [the longest x1 19.2 us: attention(): pl.pallas_call(attention_kernel, out_shape=(jax.ShapeDtypeStruct((rows, h...]
    gather x13 -> x0, local copies, waits for them, and re-layouts: 26 us -> none  [the longest x1 5.21 us: body(): jnp.take(returned.reshape(-1, model_width), slot_index, axis=0)]
    reshape x4 -> x0, local copies, waits for them, and re-layouts: 8.26 us -> none  [the longest x1 4.12 us: body(): outgoing = outgoing.reshape(devices, local_experts, capacity, model_width)]
    reduce_sum x9 -> x3, other arithmetic: 8.92 us -> 1.71 us  [the longest x1 1.14 us: body(): jnp.mean(hidden32 * hidden32, axis=-1, keepdims=True) + EPSILON]
  transfers between devices with their start and end apart: 5 -> 7, of which waited for: 2 -> 5; matrix products, arithmetic and copies ran while one was open for 24% -> 2% of each run, Pallas kernels for 0% -> 0%
where the time goes in v1:
time: 160 us; the launch traced here: 159 us
  waiting for transfers between devices  48.7 us (30%)
  blocking collectives  42.5 us (27%)
  Pallas kernels  26.8 us (17%)
  local copies, waits for them, and re-layouts  17.2 us (11%)
  starting transfers between devices  15.8 us (10%)
  other arithmetic  5.54 us (3%)
    all_to_all x1, blocking collectives, body(): lax.all_to_all(outgoing, ('req', 'kv'), split_axis=0, concat_axis=0, tile...  42.5 us
    ppermute x1, waiting for transfers between devices, body(): arrived_keys = lax.ppermute(depart_keys, 'req', swap)  33.1 us
    pallas_call x1, Pallas kernels, attention(): pl.pallas_call(attention_kernel, out_shape=(jax.ShapeDtypeStruct((rows, h...  19.2 us
    unnamed x30, local copies, waits for them, and re-layouts  15.5 us
    ppermute x1, waiting for transfers between devices, body(): arrived_values = lax.ppermute(depart_values, 'req', swap)  11.2 us
    pallas_call x1, Pallas kernels, expert(): pl.pallas_call(expert_kernel, out_shape=jax.ShapeDtypeStruct((rows, half)...  6.41 us
    ppermute x3, starting transfers between devices, body(): total = total + lax.ppermute(block, 'kv', ring).astype(F32)  5.74 us
    ppermute x3, waiting for transfers between devices, body(): total = total + lax.ppermute(block, 'kv', ring).astype(F32)  4.35 us
  transfers between devices with their start and end apart: 7, of which 5 were waited for; matrix products, arithmetic and copies ran while one was open for 2% of the time, Pallas kernels for 0%

profile of v1, /device:TPU:1, one launch (start us, length us, event | category | flops | bytes accessed | tf_op | source)
XLA Modules:
  0.0 158.7 jit_solution(2367876132243004214)
XLA Ops:
  0.7 0.8 copy.31.table
  1.5 0.8 fusion.40
  2.2 0.3 fusion.19
  2.5 0.9 fusion.41
  3.4 0.1 pad_maximum_fusion
  3.5 0.0 copy-start
  3.5 2.7 %copy-done = bf16[368,1,64,128]{3,2,1,0:T(8,128)(2,1)S(1)} copy-done((bf16[368,1,64,128]{3,2,1,0:T(8,128)(2,1)S(1)}, bf16[368,1,64,128]{3,2,1,0:T(8,128)(2,1)}, u32[]{:S(2)}) %copy-start) | copy-done | bytes 6029336
  6.2 0.0 copy-start.2
  6.2 2.2 %copy-done.2 = bf16[2048,1024]{1,0:T(8,128)(2,1)S(1)} copy-done((bf16[2048,1024]{1,0:T(8,128)(2,1)S(1)}, bf16[2048,1024]{1,0:T(8,128)(2,1)}, u32[]{:S(2)}) %copy-start.2) | copy-done | bytes 4194328
  8.4 0.0 copy-start.6
  8.4 1.0 copy-done.6
  9.5 0.0 copy-start.7
  9.5 1.0 copy-done.7
  10.5 1.0 copy-done.8
  11.5 0.0 copy-start.9
  11.5 0.7 copy-done.9
  12.2 0.0 copy-start.12
  12.2 19.2 %attention.1 = (bf16[128,1024]{1,0:T(8,128)(2,1)S(1)}, bf16[48,128]{1,0:T(8,128)(2,1)S(1)}, bf16[2,1024,128]{2,1,0:T(8,128)(2,1)S(1)}, bf16[2,1024,128]{2,1,0:T(8,128)(2,1)S(1)}) custom-call(s32[128,16]{1,0:T(8,128)S(1)} %copy.31.table, s32[128]{0:T(128)S(1)} %get-tuple-element.25.lens, s32[2]{0:T(128)S(1)} %get-tuple-element.26.slots, ...), custom_call_target="tpu_custom_call" | custom-call | tf_op jit(solution)/shard_map/attention/pallas_call | solution.py:224
  31.4 3.1 %collective-permute-start = (bf16[48,128]{1,0:T(8,128)(2,1)S(1)}, bf16[48,128]{1,0:T(8,128)(2,1)S(1)}, u32[]{:S(2)}, u32[]{:S(2)}) collective-permute-start(bf16[48,128]{1,0:T(8,128)(2,1)S(1)} %get-tuple-element.7), channel_id=1, source_target_pairs={{0,64},{4,68},{8,72},{12,76},{16,80},{20,84},{24,88},{28,92},{32,9... | collective-permute-start | bytes 36872 | tf_op jit(solution)/shard_map/ppermute | solution.py:367
  34.5 0.5 fusion.44
  35.1 0.0 copy-done.12
  35.1 0.1 copy.32
  35.1 0.1 eq.86
  35.2 0.2 convert_reduce_fusion
  35.4 0.1 reduce_sum.39
  35.5 0.4 compare_reduce_fusion
  36.0 1.3 fusion.35
  37.3 0.0 collective-permute-done.arrived
  37.3 0.0 copy-start.1
  37.3 2.2 %copy-done.1 = bf16[1024,2048]{1,0:T(8,128)(2,1)S(1)} copy-done((bf16[1024,2048]{1,0:T(8,128)(2,1)S(1)}, bf16[1024,2048]{1,0:T(8,128)(2,1)}, u32[]{:S(2)}) %copy-start.1) | copy-done | bytes 4194328
  39.5 0.0 copy-start.11
  39.5 0.0 copy-start.5
  39.5 1.3 project.1
  40.8 1.7 %collective-permute-start.1 = (bf16[32,2048]{1,0:T(8,128)(2,1)S(1)}, bf16[32,2048]{1,0:T(8,128)(2,1)S(1)}, u32[]{:S(2)}, u32[]{:S(2)}) collective-permute-start(bf16[32,2048]{1,0:T(8,128)(2,1)S(1)} %get-tuple-element.28), channel_id=1, source_target_pairs={{0,1},{1,2},{2,3},{3,0},{4,5},{5,6},{6,7},{7,4},{8,9},{9,10},{10,1... | collective-permute-start | bytes 393224 | tf_op jit(solution)/shard_map/ppermute | solution.py:378
  42.5 3.3 %collective-permute-start.2 = (bf16[32,2048]{1,0:T(8,128)(2,1)S(1)}, bf16[32,2048]{1,0:T(8,128)(2,1)S(1)}, u32[]{:S(2)}, u32[]{:S(2)}) collective-permute-start(bf16[32,2048]{1,0:T(8,128)(2,1)S(1)} %get-tuple-element.30), channel_id=1, source_target_pairs={{0,2},{1,3},{2,0},{3,1},{4,6},{5,7},{6,4},{7,5},{8,10},{9,11},{10,... | collective-permute-start | bytes 393224 | tf_op jit(solution)/shard_map/ppermute | solution.py:378
  45.8 0.7 collective-permute-start.3
  46.6 0.4 collective-permute-done.1
  47.0 3.3 %collective-permute-done.2 = bf16[32,2048]{1,0:T(8,128)(2,1)S(1)} collective-permute-done((bf16[32,2048]{1,0:T(8,128)(2,1)S(1)}, bf16[32,2048]{1,0:T(8,128)(2,1)S(1)}, u32[]{:S(2)}, u32[]{:S(2)}) %collective-permute-start.2) | collective-permute-done | bytes 131104 | tf_op jit(solution)/shard_map/ppermute | solution.py:378
  50.3 0.6 collective-permute-done.3
  50.9 1.1 fusion.3
  52.1 0.0 copy-done.11
  52.1 0.1 fusion.5
  52.2 0.0 copy-start.3
  52.2 0.0 copy-start.4
  52.2 0.8 convert_bitcast_fusion
  53.0 42.5 %all_to_all.10 = bf16[128,8,1024]{2,1,0:T(8,128)(2,1)S(1)} all-to-all(bf16[128,8,1024]{2,1,0:T(8,128)(2,1)S(1)} %convert_bitcast_fusion), channel_id=1, replica_groups=mesh['req'=32,'kv'=4] {'req','kv'}, dimensions={0} | all-to-all | bytes 4194304 | tf_op jit(solution)/shard_map/all_to_all | solution.py:418
  95.5 0.0 copy-done.5
  95.5 0.0 copy-done.3
  95.5 0.0 copy-done.4
  95.5 6.4 %expert.1 = bf16[1024,1024]{1,0:T(8,128)(2,1)} custom-call(bf16[1024,1024]{1,0:T(8,128)(2,1)S(1)} %bitcast.40, bf16[1,2048,768]{2,1,0:T(8,128)(2,1)S(1)} %copy-done.3, bf16[1,2048,768]{2,1,0:T(8,128)(2,1)S(1)} %copy-done.4, bf16[1,768,2048]{2,1,0:T(8,128)(2,1)S(1)} %copy-done.5), custom_call_target="tpu_custom_call" | custom-call | tf_op jit(solution)/shard_map/expert/pallas_call | solution.py:310
  101.9 0.0 copy-start.10
  101.9 3.8 %all-to-all-start.1 = ((bf16[128,8,1024]{2,1,0:T(8,128)(2,1)}), bf16[128,8,1024]{2,1,0:T(8,128)(2,1)S(1)}, u32[]{:S(2)}, u32[]{:S(2)}) async-start(bf16[128,8,1024]{2,1,0:T(8,128)(2,1)} %bitcast.15), calls=%async_computation.1 | async-start | bytes 4194304 | tf_op jit(solution)/shard_map/all_to_all | solution.py:420
  105.7 3.1 %collective-permute-start.4 = (bf16[2,1024,128]{2,1,0:T(8,128)(2,1)S(1)}, bf16[2,1024,128]{2,1,0:T(8,128)(2,1)}, u32[]{:S(2)}, u32[]{:S(2)}) collective-permute-start(bf16[2,1024,128]{2,1,0:T(8,128)(2,1)S(1)} %get-tuple-element.9), channel_id=1, source_target_pairs={{0,64},{4,68},{8,72},{12,76},{16,80},{20,84},{24,88},{28,92},{32,9... | collective-permute-start | bytes 1572872 | tf_op jit(solution)/shard_map/ppermute | solution.py:368
  108.8 0.1 collective-permute-start.5
  108.9 0.0 copy-done.10
  108.9 0.1 copy.34
  109.0 0.4 fusion.2
  109.4 33.1 %collective-permute-done.4 = bf16[2,1024,128]{2,1,0:T(8,128)(2,1)} collective-permute-done((bf16[2,1024,128]{2,1,0:T(8,128)(2,1)S(1)}, bf16[2,1024,128]{2,1,0:T(8,128)(2,1)}, u32[]{:S(2)}, u32[]{:S(2)}) %collective-permute-start.4) | collective-permute-done | bytes 524320 | tf_op jit(solution)/shard_map/ppermute | solution.py:368
  142.5 11.2 %collective-permute-done.5 = bf16[2,1024,128]{2,1,0:T(8,128)(2,1)} collective-permute-done((bf16[2,1024,128]{2,1,0:T(8,128)(2,1)S(1)}, bf16[2,1024,128]{2,1,0:T(8,128)(2,1)}, u32[]{:S(2)}, u32[]{:S(2)}) %collective-permute-start.5) | collective-permute-done | bytes 524320 | tf_op jit(solution)/shard_map/ppermute | solution.py:369
  153.8 0.0 all-to-all-done.1
  153.8 0.4 fusion
  154.3 0.7 fusion.6
  155.0 1.9 %copy.41 = bf16[2,1,1024,128]{3,2,1,0:T(8,128)(2,1)} copy(bf16[2,1,1024,128]{3,2,1,0:T(8,128)(2,1)} %bitcast.18) | data formatting | bytes 1048576
  156.8 1.9 %copy.42 = bf16[2,1,1024,128]{3,2,1,0:T(8,128)(2,1)} copy(bf16[2,1,1024,128]{3,2,1,0:T(8,128)(2,1)} %bitcast.20) | data formatting | bytes 1048576
  (17 shorter events, 0.3 us)
Async XLA Ops:
  3.5 2.7 %copy-start = (bf16[368,1,64,128]{3,2,1,0:T(8,128)(2,1)S(1)}, bf16[368,1,64,128]{3,2,1,0:T(8,128)(2,1)}, u32[]{:S(2)}) copy-start(bf16[368,1,64,128]{3,2,1,0:T(8,128)(2,1)} %k_hbm.1) | copy-start | bytes 18087940
  6.2 2.2 %copy-start.2 = (bf16[2048,1024]{1,0:T(8,128)(2,1)S(1)}, bf16[2048,1024]{1,0:T(8,128)(2,1)}, u32[]{:S(2)}) copy-start(bf16[2048,1024]{1,0:T(8,128)(2,1)} %wq_hbm.1) | copy-start | bytes 12582916
  8.4 1.0 copy-start.6
  9.5 1.0 copy-start.7
  10.5 1.0 copy-start.8
  11.5 0.7 copy-start.9
  12.2 22.8 %copy-start.12 = (s32[32,8]{0,1:T(8,128)S(1)}, s32[32,8]{0,1:T(8,128)}, u32[]{:S(2)}) copy-start(s32[32,8]{0,1:T(8,128)} %param.29) | copy-start | bytes 3076
  31.4 5.9 %collective-permute-start = (bf16[48,128]{1,0:T(8,128)(2,1)S(1)}, bf16[48,128]{1,0:T(8,128)(2,1)S(1)}, u32[]{:S(2)}, u32[]{:S(2)}) collective-permute-start(bf16[48,128]{1,0:T(8,128)(2,1)S(1)} %get-tuple-element.7), channel_id=1, source_target_pairs={{0,64},{4,68},{8,72},{12,76},{16,80},{20,84},{24,88},{28,92},{32,9... | collective-permute-start | bytes 36872 | tf_op jit(solution)/shard_map/ppermute | solution.py:367
  37.3 2.2 %copy-start.1 = (bf16[1024,2048]{1,0:T(8,128)(2,1)S(1)}, bf16[1024,2048]{1,0:T(8,128)(2,1)}, u32[]{:S(2)}) copy-start(bf16[1024,2048]{1,0:T(8,128)(2,1)} %w_out.1) | copy-start | bytes 12582916
  39.5 12.6 %copy-start.11 = (f32[2048]{0:T(1024)S(1)}, f32[2048]{0:T(1024)}, u32[]{:S(2)}) copy-start(f32[2048]{0:T(1024)} %param.28) | copy-start | bytes 24580
  39.5 56.0 %copy-start.5 = (bf16[1,768,2048]{2,1,0:T(8,128)(2,1)S(1)}, bf16[1,768,2048]{2,1,0:T(8,128)(2,1)}, u32[]{:S(2)}) copy-start(bf16[1,768,2048]{2,1,0:T(8,128)(2,1)} %wd.1) | copy-start | bytes 9437188
  40.8 6.2 %collective-permute-start.1 = (bf16[32,2048]{1,0:T(8,128)(2,1)S(1)}, bf16[32,2048]{1,0:T(8,128)(2,1)S(1)}, u32[]{:S(2)}, u32[]{:S(2)}) collective-permute-start(bf16[32,2048]{1,0:T(8,128)(2,1)S(1)} %get-tuple-element.28), channel_id=1, source_target_pairs={{0,1},{1,2},{2,3},{3,0},{4,5},{5,6},{6,7},{7,4},{8,9},{9,10},{10,1... | collective-permute-start | bytes 393224 | tf_op jit(solution)/shard_map/ppermute | solution.py:378
  42.5 7.7 %collective-permute-start.2 = (bf16[32,2048]{1,0:T(8,128)(2,1)S(1)}, bf16[32,2048]{1,0:T(8,128)(2,1)S(1)}, u32[]{:S(2)}, u32[]{:S(2)}) collective-permute-start(bf16[32,2048]{1,0:T(8,128)(2,1)S(1)} %get-tuple-element.30), channel_id=1, source_target_pairs={{0,2},{1,3},{2,0},{3,1},{4,6},{5,7},{6,4},{7,5},{8,10},{9,11},{10,... | collective-permute-start | bytes 393224 | tf_op jit(solution)/shard_map/ppermute | solution.py:378
  45.8 5.1 %collective-permute-start.3 = (bf16[32,2048]{1,0:T(8,128)(2,1)S(1)}, bf16[32,2048]{1,0:T(8,128)(2,1)S(1)}, u32[]{:S(2)}, u32[]{:S(2)}) collective-permute-start(bf16[32,2048]{1,0:T(8,128)(2,1)S(1)} %get-tuple-element.29), channel_id=1, source_target_pairs={{0,3},{1,0},{2,1},{3,2},{4,7},{5,4},{6,5},{7,6},{8,11},{9,8},{10,9... | collective-permute-start | bytes 393224 | tf_op jit(solution)/shard_map/ppermute | solution.py:378
  52.2 43.3 %copy-start.3 = (bf16[1,2048,768]{2,1,0:T(8,128)(2,1)S(1)}, bf16[1,2048,768]{2,1,0:T(8,128)(2,1)}, u32[]{:S(2)}) copy-start(bf16[1,2048,768]{2,1,0:T(8,128)(2,1)} %wg.1) | copy-start | bytes 9437188
  52.2 43.3 %copy-start.4 = (bf16[1,2048,768]{2,1,0:T(8,128)(2,1)S(1)}, bf16[1,2048,768]{2,1,0:T(8,128)(2,1)}, u32[]{:S(2)}) copy-start(bf16[1,2048,768]{2,1,0:T(8,128)(2,1)} %wu.1) | copy-start | bytes 9437188
  101.9 7.0 %copy-start.10 = (f32[32,8]{0,1:T(8,128)S(1)}, f32[32,8]{0,1:T(8,128)}, u32[]{:S(2)}) copy-start(f32[32,8]{0,1:T(8,128)} %param.30) | copy-start | bytes 3076
  101.9 51.9 %all-to-all-start.1 = ((bf16[128,8,1024]{2,1,0:T(8,128)(2,1)}), bf16[128,8,1024]{2,1,0:T(8,128)(2,1)S(1)}, u32[]{:S(2)}, u32[]{:S(2)}) async-start(bf16[128,8,1024]{2,1,0:T(8,128)(2,1)} %bitcast.15), calls=%async_computation.1 | async-start | bytes 4194304 | tf_op jit(solution)/shard_map/all_to_all | solution.py:420
  105.7 36.8 %collective-permute-start.4 = (bf16[2,1024,128]{2,1,0:T(8,128)(2,1)S(1)}, bf16[2,1024,128]{2,1,0:T(8,128)(2,1)}, u32[]{:S(2)}, u32[]{:S(2)}) collective-permute-start(bf16[2,1024,128]{2,1,0:T(8,128)(2,1)S(1)} %get-tuple-element.9), channel_id=1, source_target_pairs={{0,64},{4,68},{8,72},{12,76},{16,80},{20,84},{24,88},{28,92},{32,9... | collective-permute-start | bytes 1572872 | tf_op jit(solution)/shard_map/ppermute | solution.py:368
  108.8 45.0 %collective-permute-start.5 = (bf16[2,1024,128]{2,1,0:T(8,128)(2,1)S(1)}, bf16[2,1024,128]{2,1,0:T(8,128)(2,1)}, u32[]{:S(2)}, u32[]{:S(2)}) collective-permute-start(bf16[2,1024,128]{2,1,0:T(8,128)(2,1)S(1)} %get-tuple-element.10), channel_id=1, source_target_pairs={{0,64},{4,68},{8,72},{12,76},{16,80},{20,84},{24,88},{28,92},{32,9... | collective-permute-start | bytes 1572872 | tf_op jit(solution)/shard_map/ppermute | solution.py:369

commit v2 on v1

v2 whole, which is shorter than its diff:
```python
import math

import jax
import jax.numpy as jnp
from jax import lax
from jax.experimental import pallas as pl
from jax.experimental.pallas import tpu as pltpu
from jax.sharding import PartitionSpec as P

EPSILON = 1e-06
THETA = 1000000.0
MASKED = -1e30
BF16 = jnp.bfloat16
F32 = jnp.float32
POOL_CUTS = 4
QUERY_CUTS = 4
OUT_CUTS = 4
GROUP = 4
UNROLL_SHORT = 8
UNROLL_LONG = 4


def dot_t(a, b):
    return lax.dot_general(a, b, (((1,), (1,)), ((), ())), preferred_element_type=F32)


def dot_n(a, b):
    return jnp.dot(a, b, preferred_element_type=F32)


def in_hbm(x):
    return pltpu.with_memory_space_constraint(x, pltpu.HBM)


def attention_kernel(
    table_hbm,
    lens_hbm,
    slots_hbm,
    tokens_hbm,
    gain_hbm,
    wq_hbm,
    wk_hbm,
    wv_hbm,
    k_hbm,
    v_hbm,
    att_out,
    mig_out,
    dk_out,
    dv_out,
    table,
    lens,
    lens_row,
    slots,
    tokens,
    gain,
    wq,
    wk,
    wv,
    kp,
    vp,
    qs,
    ks,
    vs,
    os,
    mig,
    longs,
    isem,
    wsem,
    psem,
):
    rows, width = tokens.shape
    pool, page, head = kp.shape
    max_pages = table.shape[0]
    heads = wq.shape[1] // head
    scale = 1.0 / math.sqrt(head)
    wcut = wq.shape[1] // QUERY_CUTS
    pcut = pool // POOL_CUTS
    req = lax.axis_index("req")

    icopies = [
        pltpu.make_async_copy(tokens_hbm, tokens, isem.at[0]),
        pltpu.make_async_copy(gain_hbm, gain, isem.at[1]),
        pltpu.make_async_copy(lens_hbm.at[pl.ds(req, 1)], lens_row, isem.at[2]),
        pltpu.make_async_copy(lens_hbm.at[pl.ds(req, 1)], lens, isem.at[3]),
        pltpu.make_async_copy(table_hbm, table, isem.at[4]),
        pltpu.make_async_copy(slots_hbm, slots, isem.at[5]),
    ]
    wcopies = [
        pltpu.make_async_copy(
            wq_hbm.at[:, pl.ds(c * wcut, wcut)], wq.at[:, pl.ds(c * wcut, wcut)], wsem.at[c]
        )
        for c in range(QUERY_CUTS)
    ]
    wcopies.append(pltpu.make_async_copy(wk_hbm, wk, wsem.at[QUERY_CUTS]))
    wcopies.append(pltpu.make_async_copy(wv_hbm, wv, wsem.at[QUERY_CUTS + 1]))
    pcopies = []
    for i, (src, dst) in enumerate(((k_hbm, kp), (v_hbm, vp))):
        for c in range(POOL_CUTS):
            pcopies.append(
                pltpu.make_async_copy(
                    src.at[pl.ds(c * pcut, pcut), 0],
                    dst.at[pl.ds(c * pcut, pcut)],
                    psem.at[i * POOL_CUTS + c],
                )
            )
    for copy in icopies + wcopies + pcopies:
        copy.start()
    for copy in icopies:
        copy.wait()

    def gather_long(r, n):
        is_long = lens[0, r] > page

        @pl.when(is_long)
        def _():
            longs[n] = r

        return n + is_long.astype(jnp.int32)

    long_count = lax.fori_loop(0, rows, gather_long, jnp.int32(0))

    positions = jnp.broadcast_to(lens_row[...], (rows, rows)).astype(F32).T
    half_lane = lax.broadcasted_iota(jnp.int32, (1, head), 1)
    exponent = (half_lane % (head // 2)).astype(F32) * (-2.0 / head)
    angles = positions * jnp.exp(exponent * math.log(THETA))
    cos = jnp.cos(angles)
    sin = jnp.where(half_lane < head // 2, -1.0, 1.0) * jnp.sin(angles)

    x = tokens[...].astype(F32)
    row_id = lax.broadcasted_iota(jnp.int32, (rows, 1), 0)
    for k in range(2):
        leaving = jnp.sum(jnp.where(row_id == slots[k, req], x, 0.0), axis=0, keepdims=True)
        for c in range(width // head):
            mig[k * 24 + 8 + c : k * 24 + 9 + c, :] = leaving[:, c * head : (c + 1) * head]
    normed = (
        x * lax.rsqrt(jnp.mean(x * x, axis=-1, keepdims=True) + EPSILON) * gain[...]
    ).astype(BF16)

    def rotated(vectors):
        unit = vectors * lax.rsqrt(jnp.mean(vectors * vectors, axis=-1, keepdims=True) + EPSILON)
        turned = unit * cos + pltpu.roll(unit, head // 2, 1) * sin
        return turned.astype(BF16).astype(F32)

    per_cut = wcut // head
    for c in range(QUERY_CUTS):
        wcopies[c].wait()
        query = dot_n(normed, wq[:, c * wcut : (c + 1) * wcut])
        for i in range(per_cut):
            qs[pl.ds(c * per_cut + i, rows, stride=heads), :] = rotated(
                query[:, i * head : (i + 1) * head]
            )
    wcopies[QUERY_CUTS].wait()
    wcopies[QUERY_CUTS + 1].wait()
    fresh_key = rotated(dot_n(normed, wk[...]))
    fresh_value = dot_n(normed, wv[...]).astype(BF16).astype(F32)
    for h in range(heads):
        ks[pl.ds(h, rows, stride=heads), :] = fresh_key
        vs[pl.ds(h, rows, stride=heads), :] = fresh_value

    for copy in pcopies:
        copy.wait()

    def finish(bases, queries, scores, valids, values):
        count = queries[0].shape[0]
        scores = [jnp.where(v, x * scale, MASKED) for v, x in zip(valids, scores)]
        selves = [
            jnp.sum(q * ks[pl.ds(b, count), :], axis=1, keepdims=True) * scale
            for b, q in zip(bases, queries)
        ]
        tops = [
            jnp.maximum(jnp.max(x, axis=1, keepdims=True), y) for x, y in zip(scores, selves)
        ]
        weights = [jnp.exp(x - t) for x, t in zip(scores, tops)]
        summed = [dot_n(w.astype(BF16), v()) for w, v in zip(weights, values)]
        selves = [jnp.exp(y - t) for y, t in zip(selves, tops)]
        totals = [jnp.sum(w, axis=1, keepdims=True) + y for w, y in zip(weights, selves)]
        for b, y, t, o in zip(bases, selves, totals, summed):
            fresh = y.astype(BF16).astype(F32) * vs[pl.ds(b, count), :]
            os[pl.ds(b, count), :] = (o + fresh) / t

    lanes = lax.broadcasted_iota(jnp.int32, (GROUP * heads, GROUP * page), 1)
    subs = lax.broadcasted_iota(jnp.int32, (GROUP * heads, GROUP * page), 0)
    place = jnp.where(lanes // page == subs // heads, lanes % page, 1 << 20)
    lane_row = lax.broadcasted_iota(jnp.int32, (1, GROUP * page), 1)

    def joined(pool_ref, pages):
        return jnp.concatenate([pool_ref[p] for p in pages], axis=0)

    def short_step(step, carry):
        firsts = [(step * UNROLL_SHORT + u) * GROUP for u in range(UNROLL_SHORT)]
        bases = [pl.multiple_of(f * heads, GROUP * heads) for f in firsts]
        pages = [[table[0, f + i] for i in range(GROUP)] for f in firsts]
        queries = [qs[pl.ds(b, GROUP * heads), :] for b in bases]
        scores = [dot_t(q.astype(BF16), joined(kp, p)) for q, p in zip(queries, pages)]
        valids = []
        for f in firsts:
            limit = jnp.full((1, GROUP * page), lens[0, f], jnp.int32)
            for i in range(1, GROUP):
                limit = jnp.where(lane_row >= i * page, lens[0, f + i], limit)
            valids.append(place < limit)
        finish(bases, queries, scores, valids, [lambda p=p: joined(vp, p) for p in pages])
        return carry

    lax.fori_loop(0, rows // (GROUP * UNROLL_SHORT), short_step, 0)

    span = lax.broadcasted_iota(jnp.int32, (heads, max_pages * page), 1)

    def long_step(step, carry):
        who = [longs[jnp.minimum(step * UNROLL_LONG + u, long_count - 1)] for u in range(UNROLL_LONG)]
        bases = [pl.multiple_of(r * heads, heads) for r in who]
        pages = [[table[j, r] for j in range(max_pages)] for r in who]
        queries = [qs[pl.ds(b, heads), :] for b in bases]
        scores = []
        for q, p in zip(queries, pages):
            q16 = q.astype(BF16)
            parts = [dot_t(q16, joined(kp, p[c : c + 4])) for c in range(0, max_pages, 4)]
            scores.append(jnp.concatenate(parts, axis=1))
        valids = [span < lens[0, r] for r in who]
        finish(bases, queries, scores, valids, [lambda p=p: joined(vp, p) for p in pages])
        return carry

    lax.fori_loop(0, (long_count + UNROLL_LONG - 1) // UNROLL_LONG, long_step, 0)

    for h in range(heads):
        att_out[:, h * head : (h + 1) * head] = os[pl.ds(h, rows, stride=heads), :].astype(BF16)
    for k in range(2):
        mig[k * 24 : k * 24 + 8, :] = os[pl.ds(pl.multiple_of(slots[k, req] * heads, heads), heads), :]
    mig_out[...] = mig[...].astype(BF16)
    for k in range(2):

        def depart(j, carry, k=k):
            held = table[j, slots[k, req]]
            at = pl.multiple_of(j * page, page)
            dk_out[k, pl.ds(at, page), :] = kp[held]
            dv_out[k, pl.ds(at, page), :] = vp[held]
            return carry

        lax.fori_loop(0, max_pages, depart, 0)


def attention(table, lens, slots, tokens, gain, wq, wk, wv, kc, vc):
    rows, _ = tokens.shape
    pool, _, page, head = kc.shape
    heads = wq.shape[1] // head
    span = table.shape[0] * page
    vmem = pl.BlockSpec(memory_space=pltpu.VMEM)
    hbm = pl.BlockSpec(memory_space=pltpu.HBM)
    return pl.pallas_call(
        attention_kernel,
        out_shape=(
            jax.ShapeDtypeStruct((rows, heads * head), BF16),
            jax.ShapeDtypeStruct((48, head), BF16),
            jax.ShapeDtypeStruct((2, span, head), BF16),
            jax.ShapeDtypeStruct((2, span, head), BF16),
        ),
        in_specs=[hbm] * 10,
        out_specs=(vmem,) * 4,
        scratch_shapes=[
            pltpu.SMEM(table.shape, jnp.int32),
            pltpu.SMEM((1, rows), jnp.int32),
            pltpu.VMEM((1, rows), jnp.int32),
            pltpu.SMEM(slots.shape, jnp.int32),
            pltpu.VMEM(tokens.shape, BF16),
            pltpu.VMEM(gain.shape, F32),
            pltpu.VMEM(wq.shape, BF16),
            pltpu.VMEM(wk.shape, BF16),
            pltpu.VMEM(wv.shape, BF16),
            pltpu.VMEM((pool, page, head), BF16),
            pltpu.VMEM((pool, page, head), BF16),
            pltpu.VMEM((rows * heads, head), F32),
            pltpu.VMEM((rows * heads, head), F32),
            pltpu.VMEM((rows * heads, head), F32),
            pltpu.VMEM((rows * heads, head), F32),
            pltpu.VMEM((48, head), F32),
            pltpu.SMEM((rows,), jnp.int32),
            pltpu.SemaphoreType.DMA((6,)),
            pltpu.SemaphoreType.DMA((QUERY_CUTS + 2,)),
            pltpu.SemaphoreType.DMA((2 * POOL_CUTS,)),
        ],
        compiler_params=pltpu.CompilerParams(vmem_limit_bytes=36 << 20),
        name="attention",
    )(*map(in_hbm, (table, lens, slots, tokens, gain, wq, wk, wv, kc, vc)))


def project_kernel(slots_hbm, attended, arrived, w_hbm, *rest):
    outs, (slots, w_out, partial, sem) = rest[:-4], rest[-4:]
    load = pltpu.make_async_copy(slots_hbm, slots, sem.at[0])
    load.start()
    cut = w_hbm.shape[1] // OUT_CUTS
    loads = []
    for c in range(OUT_CUTS):
        span = pl.ds(c * cut, cut)
        loads.append(pltpu.make_async_copy(w_hbm.at[:, span], w_out.at[:, span], sem.at[c + 1]))
        loads[-1].start()
    rows, _ = attended.shape
    block = rows // len(outs)
    head = arrived.shape[1]
    heads = attended.shape[1] // head
    row_id = lax.broadcasted_iota(jnp.int32, (rows, head), 0)
    got = arrived[...].astype(F32)
    req = lax.axis_index("req")
    kv = lax.axis_index("kv")
    load.wait()
    pieces = []
    for h in range(heads):
        piece = attended[:, h * head : (h + 1) * head].astype(F32)
        for k in range(2):
            piece = jnp.where(row_id == slots[k, req], got[k * 24 + h : k * 24 + h + 1, :], piece)
        pieces.append(piece.astype(BF16))
    settled = jnp.concatenate(pieces, axis=1)
    for c in range(OUT_CUTS):
        loads[c].wait()
        span = slice(c * cut, (c + 1) * cut)
        partial[:, span] = dot_n(settled, w_out[:, span]).astype(BF16)
    for s, out in enumerate(outs):
        at = lax.rem(kv + s, len(outs)) * block
        out[...] = partial[pl.ds(pl.multiple_of(at, block), block), :]


def project(slots, attended, arrived, w_out, count):
    vmem = pl.BlockSpec(memory_space=pltpu.VMEM)
    hbm = pl.BlockSpec(memory_space=pltpu.HBM)
    rows, width = attended.shape[0], w_out.shape[1]
    return pl.pallas_call(
        project_kernel,
        out_shape=[jax.ShapeDtypeStruct((rows // count, width), BF16)] * count,
        in_specs=[hbm, vmem, vmem, hbm],
        out_specs=[vmem] * count,
        scratch_shapes=[
            pltpu.SMEM(slots.shape, jnp.int32),
            pltpu.VMEM(w_out.shape, BF16),
            pltpu.VMEM((rows, width), BF16),
            pltpu.SemaphoreType.DMA((OUT_CUTS + 1,)),
        ],
        compiler_params=pltpu.CompilerParams(vmem_limit_bytes=16 << 20),
        name="project",
    )(in_hbm(slots), attended, arrived, in_hbm(w_out))


def scatter_kernel(
    slots_hbm,
    tokens_hbm,
    gain_hbm,
    own,
    one,
    two,
    three,
    arrived,
    hits,
    hidden,
    out,
    slots,
    tokens,
    gain,
    isem,
):
    rows, width = own.shape
    half = width // 2
    head = arrived.shape[1]
    req = lax.axis_index("req")
    at = lax.axis_index("kv") * rows
    loads = [
        pltpu.make_async_copy(slots_hbm, slots, isem.at[0]),
        pltpu.make_async_copy(
            tokens_hbm.at[pl.ds(pl.multiple_of(at, rows), rows)], tokens, isem.at[1]
        ),
        pltpu.make_async_copy(gain_hbm, gain, isem.at[2]),
    ]
    for load in loads:
        load.start()
    total = own[...].astype(F32)
    for other in (one, two, three):
        total = total + other[...].astype(F32)
    got = arrived[...].astype(F32)
    row_id = lax.broadcasted_iota(jnp.int32, (rows, 1), 0) + at
    for load in loads:
        load.wait()
    residual = tokens[...].astype(F32)
    for k in range(2):
        row = jnp.concatenate(
            [got[k * 24 + 8 + c : k * 24 + 9 + c, :] for c in range(width // head)], axis=1
        )
        residual = jnp.where(row_id == slots[k, req], row, residual)
    settled = (residual + total).astype(BF16)
    hidden[...] = settled
    x = settled.astype(F32)
    moe_in = (
        x * lax.rsqrt(jnp.mean(x * x, axis=-1, keepdims=True) + EPSILON) * gain[...]
    ).astype(BF16)
    stacked = jnp.concatenate([moe_in[:, :half], moe_in[:, half:]], axis=0)
    cut = 256
    for c in range(out.shape[0] // cut):
        span = pl.ds(c * cut, cut)
        out[span, :] = dot_n(hits[span, :], stacked).astype(BF16)


def scatter(slots, tokens, gain, blocks, arrived, hits):
    vmem = pl.BlockSpec(memory_space=pltpu.VMEM)
    hbm = pl.BlockSpec(memory_space=pltpu.HBM)
    rows, width = blocks[0].shape
    places = hits.shape[0]
    return pl.pallas_call(
        scatter_kernel,
        out_shape=(
            jax.ShapeDtypeStruct((rows, width), BF16),
            jax.ShapeDtypeStruct((places, width // 2), BF16),
        ),
        in_specs=[hbm] * 3 + [vmem] * 6,
        out_specs=(vmem, vmem),
        scratch_shapes=[
            pltpu.SMEM(slots.shape, jnp.int32),
            pltpu.VMEM((rows, width), BF16),
            pltpu.VMEM(gain.shape, F32),
            pltpu.SemaphoreType.DMA((3,)),
        ],
        compiler_params=pltpu.CompilerParams(vmem_limit_bytes=16 << 20),
        name="scatter",
    )(in_hbm(slots), in_hbm(tokens), in_hbm(gain), *blocks, arrived, hits)


def expert_kernel(received, wg, wu, wd, out, xs, made, osem):
    pairs = received.shape[0] // 16
    half = received.shape[1]
    cut = 256
    low = lax.broadcasted_iota(jnp.int32, (pairs, 8, cut), 1) < 4
    for c in range(half // cut):
        part = received[:, c * cut : (c + 1) * cut].astype(F32).reshape(pairs, 2, 8, cut)
        one, two = part[:, 0], part[:, 1]
        left = jnp.where(low, one, pltpu.roll(two, 4, 1))
        right = jnp.where(low, pltpu.roll(one, 4, 1), two)
        xs[:, c * cut : (c + 1) * cut] = left.reshape(pairs * 8, cut).astype(BF16)
        xs[:, half + c * cut : half + (c + 1) * cut] = right.reshape(pairs * 8, cut).astype(BF16)
    inputs = xs[...]
    gate = dot_n(inputs, wg[0])
    up = dot_n(inputs, wu[0])
    act = (gate / (1.0 + jnp.exp(-gate)) * up).astype(BF16)
    copies = []
    for c in range(half // cut):
        left = dot_n(act, wd[0, :, c * cut : (c + 1) * cut]).reshape(pairs, 8, cut)
        right = dot_n(act, wd[0, :, half + c * cut : half + (c + 1) * cut]).reshape(pairs, 8, cut)
        one = jnp.where(low, left, pltpu.roll(right, 4, 1))
        two = jnp.where(low, pltpu.roll(left, 4, 1), right)
        both = jnp.stack([one, two], axis=1).reshape(pairs * 16, cut)
        span = pl.ds(c * cut, cut)
        made[:, span] = both.astype(BF16)
        copies.append(pltpu.make_async_copy(made.at[:, span], out.at[:, span], osem.at[c]))
        copies[-1].start()
    for copy in copies:
        copy.wait()


def expert(received, wg, wu, wd):
    vmem = pl.BlockSpec(memory_space=pltpu.VMEM)
    rows, half = received.shape
    return pl.pallas_call(
        expert_kernel,
        out_shape=jax.ShapeDtypeStruct((rows, half), BF16),
        in_specs=[vmem] * 4,
        out_specs=pl.BlockSpec(memory_space=pltpu.HBM),
        scratch_shapes=[
            pltpu.VMEM((rows // 2, 2 * half), BF16),
            pltpu.VMEM((rows, half), BF16),
            pltpu.SemaphoreType.DMA((half // 256,)),
        ],
        compiler_params=pltpu.CompilerParams(vmem_limit_bytes=40 << 20),
        name="expert",
    )(received, wg, wu, wd)


def settle_kernel(
    lens_hbm,
    slots_hbm,
    keys,
    values,
    keys_out,
    values_out,
    lens,
    slots,
    sem,
):
    reqs = lens_hbm.shape[0]
    partner = lax.rem(lax.axis_index("req") + reqs // 2, reqs)
    first = pltpu.make_async_copy(lens_hbm.at[pl.ds(partner, 1)], lens, sem.at[0])
    second = pltpu.make_async_copy(slots_hbm, slots, sem.at[1])
    first.start()
    second.start()
    first.wait()
    second.wait()
    cut = 256
    at = lax.broadcasted_iota(jnp.int32, (cut, keys.shape[2]), 0)
    for k in range(2):
        length = lens[0, slots[k, partner]]
        for c in range(keys.shape[1] // cut):
            keep = at < length - c * cut
            span = slice(c * cut, (c + 1) * cut)
            for src, dst in ((keys, keys_out), (values, values_out)):
                dst[k, span, :] = jnp.where(keep, src[k, span, :].astype(F32), 0.0).astype(BF16)


def settle(lens, slots, keys, values):
    vmem = pl.BlockSpec(memory_space=pltpu.VMEM)
    hbm = pl.BlockSpec(memory_space=pltpu.HBM)
    return pl.pallas_call(
        settle_kernel,
        out_shape=(
            jax.ShapeDtypeStruct(keys.shape, BF16),
            jax.ShapeDtypeStruct(values.shape, BF16),
        ),
        in_specs=[hbm] * 2 + [vmem] * 2,
        out_specs=(vmem,) * 2,
        scratch_shapes=[
            pltpu.SMEM((1, lens.shape[1]), jnp.int32),
            pltpu.SMEM(slots.shape, jnp.int32),
            pltpu.SemaphoreType.DMA((2,)),
        ],
        compiler_params=pltpu.CompilerParams(vmem_limit_bytes=20 << 20),
        name="settle",
    )(in_hbm(lens), in_hbm(slots), keys, values)


def body(
    tokens,
    lengths,
    page_table,
    key_cache,
    value_page_cache,
    mig_slot,
    attn_gain,
    w_query,
    key_weight,
    value_weight,
    w_out,
    moe_gain,
    routes,
    gate_probs,
    w_gate,
    w_up,
    w_down,
):
    req_count = lax.axis_size("req")
    kv_count = lax.axis_size("kv")
    requests_here, _ = tokens.shape
    table = page_table.T
    mig_rows = mig_slot.T
    length_rows = lengths.reshape(req_count, requests_here)
    swap = [(i, (i + req_count // 2) % req_count) for i in range(req_count)]
    attended, leaving, depart_keys, depart_values = attention(
        table,
        length_rows,
        mig_rows,
        tokens,
        attn_gain[None, :],
        w_query,
        key_weight,
        value_weight,
        key_cache,
        value_page_cache,
    )
    arrived = lax.ppermute(leaving, "req", swap)
    arrived_keys = lax.ppermute(depart_keys, "req", swap)
    arrived_values = lax.ppermute(depart_values, "req", swap)
    disp_rows = requests_here // kv_count
    blocks = list(project(mig_rows, attended, arrived, w_out, kv_count))
    for s in range(1, kv_count):
        blocks[s] = lax.ppermute(blocks[s], "kv", [(i, (i + s) % kv_count) for i in range(kv_count)])

    devices = req_count * kv_count
    top_count = routes.shape[1]
    capacity = 2 * disp_rows * top_count // devices
    flat_routes = routes.reshape(-1)
    ids = jnp.arange(disp_rows * top_count, dtype=jnp.int32)
    earlier = (flat_routes[:, None] == flat_routes[None, :]) & (ids[None, :] < ids[:, None])
    ranking = jnp.sum(earlier.astype(jnp.int32), axis=1)
    slot_index = (flat_routes * capacity + ranking).reshape(disp_rows, top_count)
    chunk_rows = 2 * capacity
    places = jnp.arange(devices * chunk_rows, dtype=jnp.int32)
    place_slot = (places // chunk_rows) * capacity + places % capacity
    place_half = (places % chunk_rows) // capacity
    stacked_slots = jnp.concatenate([slot_index, slot_index], axis=0)
    row_half = jnp.arange(2 * disp_rows, dtype=jnp.int32) // disp_rows
    hits = jnp.any(place_slot[:, None, None] == stacked_slots.T[None, :, :], axis=1)
    hits = (hits & (place_half[:, None] == row_half[None, :])).astype(BF16)
    hidden, outgoing = scatter(mig_rows, tokens, moe_gain[None, :], blocks, arrived, hits)

    shares = gate_probs / jnp.sum(gate_probs, axis=1, keepdims=True)
    stacked_shares = jnp.concatenate([shares, shares], axis=0)
    share_map = jnp.sum(
        jnp.where(
            (place_slot[None, None, :] == stacked_slots[:, :, None])
            & (place_half[None, None, :] == row_half[:, None, None]),
            stacked_shares[:, :, None],
            0.0,
        ),
        axis=1,
    )
    share_high = share_map.astype(BF16)
    share_low = (share_map - share_high.astype(F32)).astype(BF16)
    share_rows = jnp.concatenate([share_high, share_low], axis=0)

    arrived_keys, arrived_values = settle(length_rows, mig_rows, arrived_keys, arrived_values)
    received = lax.all_to_all(outgoing, ("req", "kv"), split_axis=0, concat_axis=0, tiled=True)
    made = expert(received, w_gate, w_up, w_down)
    returned = lax.all_to_all(made, ("req", "kv"), split_axis=0, concat_axis=0, tiled=True)
    mixed = dot_n(share_rows, returned)
    mixed = mixed[: 2 * disp_rows] + mixed[2 * disp_rows :]
    mixed = jnp.concatenate([mixed[:disp_rows], mixed[disp_rows:]], axis=1)
    layer_out = (hidden.astype(F32) + mixed).astype(BF16)
    return (layer_out, arrived_keys[:, None], arrived_values[:, None])


def solution(mesh):
    in_specs = (
        P("req", None),
        P(),
        P("req", None),
        P("req", "kv", None, None),
        P("req", "kv", None, None),
        P(),
        P(),
        P(None, "kv"),
        P(None, "kv"),
        P(None, "kv"),
        P("kv", None),
        P(),
        P(("req", "kv"), None),
        P(("req", "kv"), None),
        P(("req", "kv"), None, None),
        P(("req", "kv"), None, None),
        P(("req", "kv"), None, None),
    )
    out_specs = (P(("req", "kv"), None), P("req", "kv", None, None), P("req", "kv", None, None))

    return jax.shard_map(body, mesh=mesh, in_specs=in_specs, out_specs=out_specs, check_vma=False)
```

time: 160 us -> 139 us (0.87)
  local copies, waits for them, and re-layouts: 17.2 us -> 0.71 us
  other arithmetic: 5.54 us -> 2.73 us
  Pallas kernels: 26.8 us -> 24.9 us
  waiting for transfers between devices: 48.7 us -> 47 us
  starting transfers between devices: 15.8 us -> 17.5 us
    unnamed x30 -> x11, local copies, waits for them, and re-layouts: 15.5 us -> 0.11 us
    pallas_call x1, Pallas kernels: 19.2 us -> 12.5 us  [attention(): pl.pallas_call(attention_kernel, out_shape=(jax.ShapeDtypeStruct((rows, h...]
    pallas_call x1 -> x3, Pallas kernels: 1.27 us -> 6.45 us  [the longest x1 2.72 us: project(): pl.pallas_call(project_kernel, out_shape=[jax.ShapeDtypeStruct((rows // c...]
  transfers between devices with their start and end apart: 7 -> 7, of which waited for: 5 -> 5; matrix products, arithmetic and copies ran while one was open for 2% -> 2% of each run, Pallas kernels for 0% -> 1%
where the time goes in v2:
time: 139 us; the launch traced here: 138 us
  waiting for transfers between devices  47 us (34%)
  blocking collectives  42.7 us (31%)
  Pallas kernels  24.9 us (18%)
  starting transfers between devices  17.5 us (13%)
  other arithmetic  2.73 us (2%)
  matrix products  2.03 us (1%)
    all_to_all x1, blocking collectives, body(): lax.all_to_all(outgoing, ('req', 'kv'), split_axis=0, concat_axis=0, tile...  42.7 us
    ppermute x1, waiting for transfers between devices, body(): arrived_keys = lax.ppermute(depart_keys, 'req', swap)  31.7 us
    pallas_call x1, Pallas kernels, attention(): pl.pallas_call(attention_kernel, out_shape=(jax.ShapeDtypeStruct((rows, h...  12.5 us
    ppermute x1, waiting for transfers between devices, body(): arrived_values = lax.ppermute(depart_values, 'req', swap)  11.2 us
    pallas_call x1, Pallas kernels, expert(): pl.pallas_call(expert_kernel, out_shape=jax.ShapeDtypeStruct((rows, half)...  5.92 us
    ppermute x3, starting transfers between devices, body(): lax.ppermute(blocks[s], 'kv', [(i, (i + s) % kv_count) for i in range(kv_...  5.74 us
    all_to_all x1, starting transfers between devices, body(): lax.all_to_all(made, ('req', 'kv'), split_axis=0, concat_axis=0, tiled=True)  4.75 us
    ppermute x3, waiting for transfers between devices, body(): lax.ppermute(blocks[s], 'kv', [(i, (i + s) % kv_count) for i in range(kv_...  4.04 us
  transfers between devices with their start and end apart: 7, of which 5 were waited for; matrix products, arithmetic and copies ran while one was open for 2% of the time, Pallas kernels for 1%

profile of v2, /device:TPU:1, one launch (start us, length us, event | category | flops | bytes accessed | tf_op | source)
XLA Modules:
  0.0 138.3 jit_solution(16563291072081060148)
XLA Ops:
  0.6 0.0 copy-start.4
  0.6 12.5 %attention.1 = (bf16[128,1024]{1,0:T(8,128)(2,1)S(1)}, bf16[48,128]{1,0:T(8,128)(2,1)S(1)}, bf16[2,1024,128]{2,1,0:T(8,128)(2,1)S(1)}, bf16[2,1024,128]{2,1,0:T(8,128)(2,1)S(1)}) custom-call(s32[16,128]{1,0:T(8,128)} %bitcast.27, s32[32,128]{1,0:T(8,128)} %bitcast.21, s32[2,32]{1,0:T(2,128)} %bitcast.23, bf16[128,2048]{1,0:T(8,128)(2,1)} %tokens_hbm.3, ...), custom_call_target="tpu_custom_call" | custom-call | tf_op jit(solution)/shard_map/attention/pallas_call | solution.py:248
  13.1 3.8 %collective-permute-start = (bf16[48,128]{1,0:T(8,128)(2,1)S(1)}, bf16[48,128]{1,0:T(8,128)(2,1)S(1)}, u32[]{:S(2)}, u32[]{:S(2)}) collective-permute-start(bf16[48,128]{1,0:T(8,128)(2,1)S(1)} %get-tuple-element.16), channel_id=1, source_target_pairs={{0,64},{4,68},{8,72},{12,76},{16,80},{20,84},{24,88},{28,92},{32,9... | collective-permute-start | bytes 36872 | tf_op jit(solution)/shard_map/ppermute | solution.py:559
  17.0 0.0 copy-done.4
  17.0 0.1 copy.45
  17.0 0.1 eq.76
  17.1 0.2 convert_reduce_fusion
  17.3 0.1 reduce_sum.30
  17.4 0.1 copy.47
  17.5 0.3 compare_reduce_fusion
  17.9 0.3 copy.49
  18.1 0.0 collective-permute-done.arrived
  18.1 0.0 copy-start.1
  18.1 0.0 copy-start.2
  18.2 2.7 %project.1 = (bf16[32,2048]{1,0:T(8,128)(2,1)S(1)}, bf16[32,2048]{1,0:T(8,128)(2,1)S(1)}, bf16[32,2048]{1,0:T(8,128)(2,1)S(1)}, bf16[32,2048]{1,0:T(8,128)(2,1)S(1)}) custom-call(s32[2,32]{1,0:T(2,128)} %bitcast.24, bf16[128,1024]{1,0:T(8,128)(2,1)S(1)} %get-tuple-element.15.attended, bf16[48,128]{1,0:T(8,128)(2,1)S(1)} %collective-permute-done.arrived, ...), custom_call_target="tpu_custom_call" | custom-call | tf_op jit(solution)/shard_map/project/pallas_call | solution.py:324
  20.9 1.7 %collective-permute-start.1 = (bf16[32,2048]{1,0:T(8,128)(2,1)S(1)}, bf16[32,2048]{1,0:T(8,128)(2,1)S(1)}, u32[]{:S(2)}, u32[]{:S(2)}) collective-permute-start(bf16[32,2048]{1,0:T(8,128)(2,1)S(1)} %get-tuple-element.18), channel_id=1, source_target_pairs={{0,1},{1,2},{2,3},{3,0},{4,5},{5,6},{6,7},{7,4},{8,9},{9,10},{10,1... | collective-permute-start | bytes 393224 | tf_op jit(solution)/shard_map/ppermute | solution.py:565
  22.6 3.3 %collective-permute-start.2 = (bf16[32,2048]{1,0:T(8,128)(2,1)S(1)}, bf16[32,2048]{1,0:T(8,128)(2,1)S(1)}, u32[]{:S(2)}, u32[]{:S(2)}) collective-permute-start(bf16[32,2048]{1,0:T(8,128)(2,1)S(1)} %get-tuple-element.19), channel_id=1, source_target_pairs={{0,2},{1,3},{2,0},{3,1},{4,6},{5,7},{6,4},{7,5},{8,10},{9,11},{10,... | collective-permute-start | bytes 393224 | tf_op jit(solution)/shard_map/ppermute | solution.py:565
  25.9 0.7 collective-permute-start.3
  26.6 0.2 and_convert_fusion.hits
  26.8 0.2 collective-permute-done.1.one
  27.1 3.2 %collective-permute-done.2.two = bf16[32,2048]{1,0:T(8,128)(2,1)S(1)} collective-permute-done((bf16[32,2048]{1,0:T(8,128)(2,1)S(1)}, bf16[32,2048]{1,0:T(8,128)(2,1)S(1)}, u32[]{:S(2)}, u32[]{:S(2)}) %collective-permute-start.2) | collective-permute-done | bytes 131104 | tf_op jit(solution)/shard_map/ppermute | solution.py:565
  30.3 0.6 collective-permute-done.3.three
  30.9 1.8 %scatter.1 = (bf16[32,2048]{1,0:T(8,128)(2,1)S(1)}, bf16[1024,1024]{1,0:T(8,128)(2,1)S(1)}) custom-call(s32[2,32]{1,0:T(2,128)} %bitcast.25, bf16[128,2048]{1,0:T(8,128)(2,1)} %tokens_hbm.3, f32[1,2048]{1,0:T(1,128)} %bitcast.29, bf16[32,2048]{1,0:T(8,128)(2,1)S(1)} %get-tuple-element.17.own, bf16[32,2048]{1,0:T(8,128)(2,1)S(1)} %collective-permute-done.1.one, ...), custom_call_target="tpu_custom_call" | custom-call | tf_op jit(solution)/shard_map/scatter/pallas_call | solution.py:402
  32.7 0.0 copy-start
  32.7 42.7 %all_to_all.23 = bf16[128,8,1024]{2,1,0:T(8,128)(2,1)S(1)} all-to-all(bf16[128,8,1024]{2,1,0:T(8,128)(2,1)S(1)} %bitcast.20), channel_id=1, replica_groups=mesh['req'=32,'kv'=4] {'req','kv'}, dimensions={0} | all-to-all | bytes 4194304 | tf_op jit(solution)/shard_map/all_to_all | solution.py:601
  75.3 0.0 copy-done.1
  75.3 0.0 copy-done.2
  75.3 0.0 copy-done
  75.4 5.9 %expert.1 = bf16[1024,1024]{1,0:T(8,128)(2,1)} custom-call(bf16[1024,1024]{1,0:T(8,128)(2,1)S(1)} %bitcast.19, bf16[1,2048,768]{2,1,0:T(8,128)(2,1)S(1)} %copy-done, bf16[1,2048,768]{2,1,0:T(8,128)(2,1)S(1)} %copy-done.1, bf16[1,768,2048]{2,1,0:T(8,128)(2,1)S(1)} %copy-done.2), custom_call_target="tpu_custom_call" | custom-call | tf_op jit(solution)/shard_map/expert/pallas_call | solution.py:455
  81.3 0.0 copy-start.3
  81.3 4.8 %all-to-all-start.1 = ((bf16[128,8,1024]{2,1,0:T(8,128)(2,1)}), bf16[128,8,1024]{2,1,0:T(8,128)(2,1)}, u32[]{:S(2)}, u32[]{:S(2)}) async-start(bf16[128,8,1024]{2,1,0:T(8,128)(2,1)} %bitcast.8), calls=%async_computation.1 | async-start | bytes 4194304 | tf_op jit(solution)/shard_map/all_to_all | solution.py:603
  86.1 3.1 %collective-permute-start.4 = (bf16[2,1024,128]{2,1,0:T(8,128)(2,1)S(1)}, bf16[2,1024,128]{2,1,0:T(8,128)(2,1)S(1)}, u32[]{:S(2)}, u32[]{:S(2)}) collective-permute-start(bf16[2,1024,128]{2,1,0:T(8,128)(2,1)S(1)} %get-tuple-element.23), channel_id=1, source_target_pairs={{0,64},{4,68},{8,72},{12,76},{16,80},{20,84},{24,88},{28,92},{32,9... | collective-permute-start | bytes 1572872 | tf_op jit(solution)/shard_map/ppermute | solution.py:560
  89.1 0.1 collective-permute-start.5
  89.2 0.0 copy-done.3
  89.2 0.1 broadcast_compare_fusion
  89.4 0.1 pad_maximum_fusion
  89.4 0.1 copy.50
  89.5 1.0 select_reduce_fusion
  90.6 31.7 %collective-permute-done.4.keys = bf16[2,1024,128]{2,1,0:T(8,128)(2,1)S(1)} collective-permute-done((bf16[2,1024,128]{2,1,0:T(8,128)(2,1)S(1)}, bf16[2,1024,128]{2,1,0:T(8,128)(2,1)S(1)}, u32[]{:S(2)}, u32[]{:S(2)}) %collective-permute-start.4) | collective-permute-done | bytes 524320 | tf_op jit(solution)/shard_map/ppermute | solution.py:560
  122.3 11.2 %collective-permute-done.5.values = bf16[2,1024,128]{2,1,0:T(8,128)(2,1)S(1)} collective-permute-done((bf16[2,1024,128]{2,1,0:T(8,128)(2,1)S(1)}, bf16[2,1024,128]{2,1,0:T(8,128)(2,1)S(1)}, u32[]{:S(2)}, u32[]{:S(2)}) %collective-permute-start.5) | collective-permute-done | bytes 524320 | tf_op jit(solution)/shard_map/ppermute | solution.py:561
  133.5 1.9 %settle.1 = (bf16[2,1024,128]{2,1,0:T(8,128)(2,1)}, bf16[2,1024,128]{2,1,0:T(8,128)(2,1)}) custom-call(s32[32,128]{1,0:T(8,128)} %bitcast.22, s32[2,32]{1,0:T(2,128)} %bitcast.26, bf16[2,1024,128]{2,1,0:T(8,128)(2,1)S(1)} %collective-permute-done.4.keys, bf16[2,1024,128]{2,1,0:T(8,128)(2,1)S(1)} %collective-permute-done.5.values), custom_call_target="tpu_custom_call" | custom-call | tf_op jit(solution)/shard_map/settle/pallas_call | solution.py:503
  135.5 0.0 all-to-all-done.1
  135.5 2.0 %fusion = f32[128,1024]{1,0:T(8,128)S(1)} fusion(bf16[128,8,1024]{2,1,0:T(8,128)(2,1)} %all-to-all-done.1, bf16[64,1024]{1,0:T(8,128)(2,1)S(1)} %get-tuple-element.42, bf16[64,1024]{1,0:T(8,128)(2,1)S(1)} %get-tuple-element.43), kind=kOutput, calls=%fused_computation | convolution fusion | flops 268959744 | bytes 2883584 | tf_op jit(solution)/shard_map/dot_general | solution.py:28
  137.6 0.7 fusion.5
  (10 shorter events, 0.1 us)
Async XLA Ops:
  0.6 16.3 %copy-start.4 = (s32[32,8]{0,1:T(8,128)S(1)}, s32[32,8]{0,1:T(8,128)}, u32[]{:S(2)}) copy-start(s32[32,8]{0,1:T(8,128)} %param.29) | copy-start | bytes 3076
  13.1 5.0 %collective-permute-start = (bf16[48,128]{1,0:T(8,128)(2,1)S(1)}, bf16[48,128]{1,0:T(8,128)(2,1)S(1)}, u32[]{:S(2)}, u32[]{:S(2)}) collective-permute-start(bf16[48,128]{1,0:T(8,128)(2,1)S(1)} %get-tuple-element.16), channel_id=1, source_target_pairs={{0,64},{4,68},{8,72},{12,76},{16,80},{20,84},{24,88},{28,92},{32,9... | collective-permute-start | bytes 36872 | tf_op jit(solution)/shard_map/ppermute | solution.py:559
  18.1 57.2 %copy-start.1 = (bf16[1,2048,768]{2,1,0:T(8,128)(2,1)S(1)}, bf16[1,2048,768]{2,1,0:T(8,128)(2,1)}, u32[]{:S(2)}) copy-start(bf16[1,2048,768]{2,1,0:T(8,128)(2,1)} %wu.1) | copy-start | bytes 9437188
  18.1 57.2 %copy-start.2 = (bf16[1,768,2048]{2,1,0:T(8,128)(2,1)S(1)}, bf16[1,768,2048]{2,1,0:T(8,128)(2,1)}, u32[]{:S(2)}) copy-start(bf16[1,768,2048]{2,1,0:T(8,128)(2,1)} %wd.1) | copy-start | bytes 9437188
  20.9 6.2 %collective-permute-start.1 = (bf16[32,2048]{1,0:T(8,128)(2,1)S(1)}, bf16[32,2048]{1,0:T(8,128)(2,1)S(1)}, u32[]{:S(2)}, u32[]{:S(2)}) collective-permute-start(bf16[32,2048]{1,0:T(8,128)(2,1)S(1)} %get-tuple-element.18), channel_id=1, source_target_pairs={{0,1},{1,2},{2,3},{3,0},{4,5},{5,6},{6,7},{7,4},{8,9},{9,10},{10,1... | collective-permute-start | bytes 393224 | tf_op jit(solution)/shard_map/ppermute | solution.py:565
  22.6 7.7 %collective-permute-start.2 = (bf16[32,2048]{1,0:T(8,128)(2,1)S(1)}, bf16[32,2048]{1,0:T(8,128)(2,1)S(1)}, u32[]{:S(2)}, u32[]{:S(2)}) collective-permute-start(bf16[32,2048]{1,0:T(8,128)(2,1)S(1)} %get-tuple-element.19), channel_id=1, source_target_pairs={{0,2},{1,3},{2,0},{3,1},{4,6},{5,7},{6,4},{7,5},{8,10},{9,11},{10,... | collective-permute-start | bytes 393224 | tf_op jit(solution)/shard_map/ppermute | solution.py:565
  25.9 5.0 %collective-permute-start.3 = (bf16[32,2048]{1,0:T(8,128)(2,1)S(1)}, bf16[32,2048]{1,0:T(8,128)(2,1)S(1)}, u32[]{:S(2)}, u32[]{:S(2)}) collective-permute-start(bf16[32,2048]{1,0:T(8,128)(2,1)S(1)} %get-tuple-element.20), channel_id=1, source_target_pairs={{0,3},{1,0},{2,1},{3,2},{4,7},{5,4},{6,5},{7,6},{8,11},{9,8},{10,9... | collective-permute-start | bytes 393224 | tf_op jit(solution)/shard_map/ppermute | solution.py:565
  32.7 42.7 %copy-start = (bf16[1,2048,768]{2,1,0:T(8,128)(2,1)S(1)}, bf16[1,2048,768]{2,1,0:T(8,128)(2,1)}, u32[]{:S(2)}) copy-start(bf16[1,2048,768]{2,1,0:T(8,128)(2,1)} %wg.1) | copy-start | bytes 9437188
  81.3 7.9 %copy-start.3 = (f32[32,8]{0,1:T(8,128)S(1)}, f32[32,8]{0,1:T(8,128)}, u32[]{:S(2)}) copy-start(f32[32,8]{0,1:T(8,128)} %param.30) | copy-start | bytes 3076
  81.3 54.2 %all-to-all-start.1 = ((bf16[128,8,1024]{2,1,0:T(8,128)(2,1)}), bf16[128,8,1024]{2,1,0:T(8,128)(2,1)}, u32[]{:S(2)}, u32[]{:S(2)}) async-start(bf16[128,8,1024]{2,1,0:T(8,128)(2,1)} %bitcast.8), calls=%async_computation.1 | async-start | bytes 4194304 | tf_op jit(solution)/shard_map/all_to_all | solution.py:603
  86.1 36.2 %collective-permute-start.4 = (bf16[2,1024,128]{2,1,0:T(8,128)(2,1)S(1)}, bf16[2,1024,128]{2,1,0:T(8,128)(2,1)S(1)}, u32[]{:S(2)}, u32[]{:S(2)}) collective-permute-start(bf16[2,1024,128]{2,1,0:T(8,128)(2,1)S(1)} %get-tuple-element.23), channel_id=1, source_target_pairs={{0,64},{4,68},{8,72},{12,76},{16,80},{20,84},{24,88},{28,92},{32,9... | collective-permute-start | bytes 1572872 | tf_op jit(solution)/shard_map/ppermute | solution.py:560
  89.1 44.4 %collective-permute-start.5 = (bf16[2,1024,128]{2,1,0:T(8,128)(2,1)S(1)}, bf16[2,1024,128]{2,1,0:T(8,128)(2,1)S(1)}, u32[]{:S(2)}, u32[]{:S(2)}) collective-permute-start(bf16[2,1024,128]{2,1,0:T(8,128)(2,1)S(1)} %get-tuple-element.24), channel_id=1, source_target_pairs={{0,64},{4,68},{8,72},{12,76},{16,80},{20,84},{24,88},{28,92},{32,9... | collective-permute-start | bytes 1572872 | tf_op jit(solution)/shard_map/ppermute | solution.py:561

commit v3 on v2

--- a/solution.py
+++ b/solution.py
@@ -12,12 +12,13 @@
 MASKED = -1e30
 BF16 = jnp.bfloat16
 F32 = jnp.float32
-POOL_CUTS = 4
-QUERY_CUTS = 4
-OUT_CUTS = 4
+POOL_CUTS = 1
+QUERY_CUTS = 2
+OUT_CUTS = 2
+MIX_CUTS = 2
 GROUP = 4
-UNROLL_SHORT = 8
-UNROLL_LONG = 4
+UNROLL_SHORT = 16
+UNROLL_LONG = 8
 
 
 def dot_t(a, b):
@@ -45,8 +46,7 @@
     v_hbm,
     att_out,
     mig_out,
-    dk_out,
-    dv_out,
+    caches_out,
     table,
     lens,
     lens_row,
@@ -231,11 +231,11 @@
         def depart(j, carry, k=k):
             held = table[j, slots[k, req]]
             at = pl.multiple_of(j * page, page)
-            dk_out[k, pl.ds(at, page), :] = kp[held]
-            dv_out[k, pl.ds(at, page), :] = vp[held]
+            caches_out[k, pl.ds(at, page), :] = kp[held]
+            caches_out[2 + k, pl.ds(at, page), :] = vp[held]
             return carry
 
-        lax.fori_loop(0, max_pages, depart, 0)
+        lax.fori_loop(0, max_pages, depart, 0, unroll=4)
 
 
 def attention(table, lens, slots, tokens, gain, wq, wk, wv, kc, vc):
@@ -250,11 +250,10 @@
         out_shape=(
             jax.ShapeDtypeStruct((rows, heads * head), BF16),
             jax.ShapeDtypeStruct((48, head), BF16),
-            jax.ShapeDtypeStruct((2, span, head), BF16),
-            jax.ShapeDtypeStruct((2, span, head), BF16),
+            jax.ShapeDtypeStruct((4, span, head), BF16),
         ),
         in_specs=[hbm] * 10,
-        out_specs=(vmem,) * 4,
+        out_specs=(vmem,) * 3,
         scratch_shapes=[
             pltpu.SMEM(table.shape, jnp.int32),
             pltpu.SMEM((1, rows), jnp.int32),
@@ -470,8 +469,7 @@
 def settle_kernel(
     lens_hbm,
     slots_hbm,
-    keys,
-    values,
+    caches,
     keys_out,
     values_out,
     lens,
@@ -487,35 +485,73 @@
     first.wait()
     second.wait()
     cut = 256
-    at = lax.broadcasted_iota(jnp.int32, (cut, keys.shape[2]), 0)
+    at = lax.broadcasted_iota(jnp.int32, (cut, caches.shape[2]), 0)
     for k in range(2):
         length = lens[0, slots[k, partner]]
-        for c in range(keys.shape[1] // cut):
+        for c in range(caches.shape[1] // cut):
             keep = at < length - c * cut
             span = slice(c * cut, (c + 1) * cut)
-            for src, dst in ((keys, keys_out), (values, values_out)):
-                dst[k, span, :] = jnp.where(keep, src[k, span, :].astype(F32), 0.0).astype(BF16)
-
-
-def settle(lens, slots, keys, values):
+            for i, dst in enumerate((keys_out, values_out)):
+                held = caches[2 * i + k, span, :].astype(F32)
+                dst[k, span, :] = jnp.where(keep, held, 0.0).astype(BF16)
+
+
+def settle(lens, slots, caches):
     vmem = pl.BlockSpec(memory_space=pltpu.VMEM)
     hbm = pl.BlockSpec(memory_space=pltpu.HBM)
     return pl.pallas_call(
         settle_kernel,
         out_shape=(
-            jax.ShapeDtypeStruct(keys.shape, BF16),
-            jax.ShapeDtypeStruct(values.shape, BF16),
+            jax.ShapeDtypeStruct((2,) + caches.shape[1:], BF16),
+            jax.ShapeDtypeStruct((2,) + caches.shape[1:], BF16),
         ),
-        in_specs=[hbm] * 2 + [vmem] * 2,
+        in_specs=[hbm] * 2 + [vmem],
         out_specs=(vmem,) * 2,
         scratch_shapes=[
             pltpu.SMEM((1, lens.shape[1]), jnp.int32),
             pltpu.SMEM(slots.shape, jnp.int32),
             pltpu.SemaphoreType.DMA((2,)),
         ],
-        compiler_params=pltpu.CompilerParams(vmem_limit_bytes=20 << 20),
+        compiler_params=pltpu.CompilerParams(vmem_limit_bytes=4 << 20),
         name="settle",
-    )(in_hbm(lens), in_hbm(slots), keys, values)
+    )(in_hbm(lens), in_hbm(slots), caches)
+
+
+def combine_kernel(ret_hbm, high, low, hidden, out, ret, sem):
+    rows, width = hidden.shape
+    half = width // 2
+    cut = ret.shape[0] // MIX_CUTS
+    loads = []
+    for c in range(MIX_CUTS):
+        span = pl.ds(c * cut, cut)
+        loads.append(pltpu.make_async_copy(ret_hbm.at[span], ret.at[span], sem.at[c]))
+        loads[-1].start()
+    shares = jnp.concatenate([high[...], low[...]], axis=0)
+    mixed = jnp.zeros((4 * rows, half), F32)
+    for c in range(MIX_CUTS):
+        loads[c].wait()
+        span = slice(c * cut, (c + 1) * cut)
+        mixed = mixed + dot_n(shares[:, span], ret[span, :])
+    mixed = mixed[: 2 * rows] + mixed[2 * rows :]
+    kept = hidden[...].astype(F32)
+    out[:, :half] = (kept[:, :half] + mixed[:rows]).astype(BF16)
+    out[:, half:] = (kept[:, half:] + mixed[rows:]).astype(BF16)
+
+
+def combine(returned, high, low, hidden):
+    vmem = pl.BlockSpec(memory_space=pltpu.VMEM)
+    return pl.pallas_call(
+        combine_kernel,
+        out_shape=jax.ShapeDtypeStruct(hidden.shape, BF16),
+        in_specs=[pl.BlockSpec(memory_space=pltpu.HBM)] + [vmem] * 3,
+        out_specs=vmem,
+        scratch_shapes=[
+            pltpu.VMEM(returned.shape, BF16),
+            pltpu.SemaphoreType.DMA((MIX_CUTS,)),
+        ],
+        compiler_params=pltpu.CompilerParams(vmem_limit_bytes=12 << 20),
+        name="combine",
+    )(in_hbm(returned), high, low, hidden)
 
 
 def body(
@@ -544,7 +580,7 @@
     mig_rows = mig_slot.T
     length_rows = lengths.reshape(req_count, requests_here)
     swap = [(i, (i + req_count // 2) % req_count) for i in range(req_count)]
-    attended, leaving, depart_keys, depart_values = attention(
+    attended, leaving, caches = attention(
         table,
         length_rows,
         mig_rows,
@@ -557,8 +593,7 @@
         value_page_cache,
     )
     arrived = lax.ppermute(leaving, "req", swap)
-    arrived_keys = lax.ppermute(depart_keys, "req", swap)
-    arrived_values = lax.ppermute(depart_values, "req", swap)
+    caches = lax.ppermute(caches, "req", swap)
     disp_rows = requests_here // kv_count
     blocks = list(project(mig_rows, attended, arrived, w_out, kv_count))
     for s in range(1, kv_count):
@@ -595,16 +630,12 @@
     )
     share_high = share_map.astype(BF16)
     share_low = (share_map - share_high.astype(F32)).astype(BF16)
-    share_rows = jnp.concatenate([share_high, share_low], axis=0)
-
-    arrived_keys, arrived_values = settle(length_rows, mig_rows, arrived_keys, arrived_values)
+
+    arrived_keys, arrived_values = settle(length_rows, mig_rows, caches)
     received = lax.all_to_all(outgoing, ("req", "kv"), split_axis=0, concat_axis=0, tiled=True)
     made = expert(received, w_gate, w_up, w_down)
     returned = lax.all_to_all(made, ("req", "kv"), split_axis=0, concat_axis=0, tiled=True)
-    mixed = dot_n(share_rows, returned)
-    mixed = mixed[: 2 * disp_rows] + mixed[2 * disp_rows :]
-    mixed = jnp.concatenate([mixed[:disp_rows], mixed[disp_rows:]], axis=1)
-    layer_out = (hidden.astype(F32) + mixed).astype(BF16)
+    layer_out = combine(returned, share_high, share_low, hidden)
     return (layer_out, arrived_keys[:, None], arrived_values[:, None])
 
 

time: 139 us -> 134 us (0.964)
  matrix products: 2.03 us -> 0 us
    pallas_call x1, Pallas kernels: 12.5 us -> 8.98 us  [attention(): pl.pallas_call(attention_kernel, out_shape=(jax.ShapeDtypeStruct((rows, h...]
    pallas_call x1 -> x2, Pallas kernels: 1.94 us -> 4.6 us  [the longest x1 2.66 us: combine(): pl.pallas_call(combine_kernel, out_shape=jax.ShapeDtypeStruct(hidden.shap...]
    dot_general x1 -> x0, matrix products: 2.03 us -> none  [dot_n(): return jnp.dot(a, b, preferred_element_type=F32)]
    ppermute x2 -> x1, starting transfers between devices: 3.16 us -> 3.06 us  [body(): caches = lax.ppermute(caches, 'req', swap)]
    ppermute x2 -> x1, waiting for transfers between devices: 43 us -> 43 us  [body(): caches = lax.ppermute(caches, 'req', swap)]
  transfers between devices with their start and end apart: 7 -> 6, of which waited for: 5 -> 4; matrix products, arithmetic and copies ran while one was open for 2% -> 2% of each run, Pallas kernels for 1% -> 1%
where the time goes in v3:
time: 134 us
  waiting for transfers between devices  47.1 us (35%)
  blocking collectives  41.7 us (31%)
  Pallas kernels  24.2 us (18%)
  starting transfers between devices  17.4 us (13%)
  other arithmetic  2.01 us (1%)
    ppermute x1, waiting for transfers between devices, body(): caches = lax.ppermute(caches, 'req', swap)  43 us
    all_to_all x1, blocking collectives, body(): lax.all_to_all(outgoing, ('req', 'kv'), split_axis=0, concat_axis=0, tile...  41.7 us
    pallas_call x1, Pallas kernels, attention(): pl.pallas_call(attention_kernel, out_shape=(jax.ShapeDtypeStruct((rows, h...  8.98 us
    pallas_call x1, Pallas kernels, expert(): pl.pallas_call(expert_kernel, out_shape=jax.ShapeDtypeStruct((rows, half)...  5.92 us
    ppermute x3, starting transfers between devices, body(): lax.ppermute(blocks[s], 'kv', [(i, (i + s) % kv_count) for i in range(kv_...  5.74 us
    all_to_all x1, starting transfers between devices, body(): lax.all_to_all(made, ('req', 'kv'), split_axis=0, concat_axis=0, tiled=True)  4.76 us
    ppermute x3, waiting for transfers between devices, body(): lax.ppermute(blocks[s], 'kv', [(i, (i + s) % kv_count) for i in range(kv_...  4.05 us
    ppermute x1, starting transfers between devices, body(): arrived = lax.ppermute(leaving, 'req', swap)  3.81 us
  transfers between devices with their start and end apart: 6, of which 4 were waited for; matrix products, arithmetic and copies ran while one was open for 2% of the time, Pallas kernels for 1%

profile of v3, /device:TPU:1, one launch (start us, length us, event | category | flops | bytes accessed | tf_op | source)
XLA Modules:
  0.0 134.1 jit_solution(15177228266480892039)
XLA Ops:
  0.6 0.0 copy-start.4
  0.6 9.0 %attention.1 = (bf16[128,1024]{1,0:T(8,128)(2,1)S(1)}, bf16[48,128]{1,0:T(8,128)(2,1)S(1)}, bf16[4,1024,128]{2,1,0:T(8,128)(2,1)S(1)}) custom-call(s32[16,128]{1,0:T(8,128)} %bitcast.25, s32[32,128]{1,0:T(8,128)} %bitcast.19, s32[2,32]{1,0:T(2,128)} %bitcast.21, bf16[128,2048]{1,0:T(8,128)(2,1)} %tokens_hbm.3, f32[1,2048]{1,0:T(1,128)} %bitcast.26, ...), custom_call_target="tpu_custom_call" | custom-call | tf_op jit(solution)/shard_map/attention/pallas_call | solution.py:248
  9.6 3.8 %collective-permute-start = (bf16[48,128]{1,0:T(8,128)(2,1)S(1)}, bf16[48,128]{1,0:T(8,128)(2,1)S(1)}, u32[]{:S(2)}, u32[]{:S(2)}) collective-permute-start(bf16[48,128]{1,0:T(8,128)(2,1)S(1)} %get-tuple-element.15), channel_id=1, source_target_pairs={{0,64},{4,68},{8,72},{12,76},{16,80},{20,84},{24,88},{28,92},{32,9... | collective-permute-start | bytes 36872 | tf_op jit(solution)/shard_map/ppermute | solution.py:595
  13.5 0.0 copy-done.4
  13.5 0.1 copy.45
  13.5 0.1 eq.76
  13.6 0.2 convert_reduce_fusion
  13.8 0.1 reduce_sum.30
  13.9 0.1 copy.47
  14.0 0.3 compare_reduce_fusion
  14.3 0.3 copy.49
  14.6 0.0 collective-permute-done.arrived
  14.6 0.0 copy-start.1
  14.6 0.0 copy-start.2
  14.7 2.9 %project.1 = (bf16[32,2048]{1,0:T(8,128)(2,1)S(1)}, bf16[32,2048]{1,0:T(8,128)(2,1)S(1)}, bf16[32,2048]{1,0:T(8,128)(2,1)S(1)}, bf16[32,2048]{1,0:T(8,128)(2,1)S(1)}) custom-call(s32[2,32]{1,0:T(2,128)} %bitcast.22, bf16[128,1024]{1,0:T(8,128)(2,1)S(1)} %get-tuple-element.14.attended, bf16[48,128]{1,0:T(8,128)(2,1)S(1)} %collective-permute-done.arrived, ...), custom_call_target="tpu_custom_call" | custom-call | tf_op jit(solution)/shard_map/project/pallas_call | solution.py:323
  17.5 1.7 %collective-permute-start.1 = (bf16[32,2048]{1,0:T(8,128)(2,1)S(1)}, bf16[32,2048]{1,0:T(8,128)(2,1)S(1)}, u32[]{:S(2)}, u32[]{:S(2)}) collective-permute-start(bf16[32,2048]{1,0:T(8,128)(2,1)S(1)} %get-tuple-element.17), channel_id=1, source_target_pairs={{0,1},{1,2},{2,3},{3,0},{4,5},{5,6},{6,7},{7,4},{8,9},{9,10},{10,1... | collective-permute-start | bytes 393224 | tf_op jit(solution)/shard_map/ppermute | solution.py:600
  19.2 3.3 %collective-permute-start.2 = (bf16[32,2048]{1,0:T(8,128)(2,1)S(1)}, bf16[32,2048]{1,0:T(8,128)(2,1)S(1)}, u32[]{:S(2)}, u32[]{:S(2)}) collective-permute-start(bf16[32,2048]{1,0:T(8,128)(2,1)S(1)} %get-tuple-element.18), channel_id=1, source_target_pairs={{0,2},{1,3},{2,0},{3,1},{4,6},{5,7},{6,4},{7,5},{8,10},{9,11},{10,... | collective-permute-start | bytes 393224 | tf_op jit(solution)/shard_map/ppermute | solution.py:600
  22.5 0.7 collective-permute-start.3
  23.3 0.2 and_convert_fusion.hits
  23.5 0.2 collective-permute-done.1.one
  23.7 3.2 %collective-permute-done.2.two = bf16[32,2048]{1,0:T(8,128)(2,1)S(1)} collective-permute-done((bf16[32,2048]{1,0:T(8,128)(2,1)S(1)}, bf16[32,2048]{1,0:T(8,128)(2,1)S(1)}, u32[]{:S(2)}, u32[]{:S(2)}) %collective-permute-start.2) | collective-permute-done | bytes 131104 | tf_op jit(solution)/shard_map/ppermute | solution.py:600
  26.9 0.6 collective-permute-done.3.three
  27.5 1.8 %scatter.1 = (bf16[32,2048]{1,0:T(8,128)(2,1)S(1)}, bf16[1024,1024]{1,0:T(8,128)(2,1)S(1)}) custom-call(s32[2,32]{1,0:T(2,128)} %bitcast.23, bf16[128,2048]{1,0:T(8,128)(2,1)} %tokens_hbm.3, f32[1,2048]{1,0:T(1,128)} %bitcast.27, bf16[32,2048]{1,0:T(8,128)(2,1)S(1)} %get-tuple-element.16.own, bf16[32,2048]{1,0:T(8,128)(2,1)S(1)} %collective-permute-done.1.one, ...), custom_call_target="tpu_custom_call" | custom-call | tf_op jit(solution)/shard_map/scatter/pallas_call | solution.py:401
  29.3 0.0 copy-start
  29.3 41.7 %all_to_all.22 = bf16[128,8,1024]{2,1,0:T(8,128)(2,1)S(1)} all-to-all(bf16[128,8,1024]{2,1,0:T(8,128)(2,1)S(1)} %bitcast.18), channel_id=1, replica_groups=mesh['req'=32,'kv'=4] {'req','kv'}, dimensions={0} | all-to-all | bytes 4194304 | tf_op jit(solution)/shard_map/all_to_all | solution.py:635
  71.1 0.0 copy-done.1
  71.1 0.0 copy-done.2
  71.1 0.0 copy-done
  71.1 5.9 %expert.1 = bf16[1024,1024]{1,0:T(8,128)(2,1)} custom-call(bf16[1024,1024]{1,0:T(8,128)(2,1)S(1)} %bitcast.17, bf16[1,2048,768]{2,1,0:T(8,128)(2,1)S(1)} %copy-done, bf16[1,2048,768]{2,1,0:T(8,128)(2,1)S(1)} %copy-done.1, bf16[1,768,2048]{2,1,0:T(8,128)(2,1)S(1)} %copy-done.2), custom_call_target="tpu_custom_call" | custom-call | tf_op jit(solution)/shard_map/expert/pallas_call | solution.py:454
  77.0 0.0 copy-start.3
  77.0 4.8 %all-to-all-start.1 = ((bf16[128,8,1024]{2,1,0:T(8,128)(2,1)}), bf16[128,8,1024]{2,1,0:T(8,128)(2,1)}, u32[]{:S(2)}, u32[]{:S(2)}) async-start(bf16[128,8,1024]{2,1,0:T(8,128)(2,1)} %bitcast.8), calls=%async_computation.1 | async-start | bytes 4194304 | tf_op jit(solution)/shard_map/all_to_all | solution.py:637
  81.8 3.1 %collective-permute-start.4 = (bf16[4,1024,128]{2,1,0:T(8,128)(2,1)S(1)}, bf16[4,1024,128]{2,1,0:T(8,128)(2,1)S(1)}, u32[]{:S(2)}, u32[]{:S(2)}) collective-permute-start(bf16[4,1024,128]{2,1,0:T(8,128)(2,1)S(1)} %get-tuple-element.22), channel_id=1, source_target_pairs={{0,64},{4,68},{8,72},{12,76},{16,80},{20,84},{24,88},{28,92},{32,9... | collective-permute-start | bytes 3145736 | tf_op jit(solution)/shard_map/ppermute | solution.py:596
  84.9 0.0 copy-done.3
  84.9 0.1 pad_maximum_fusion
  85.0 0.1 copy.50
  85.1 0.1 broadcast_compare_fusion
  85.2 1.0 select_reduce_fusion
  86.2 43.0 %collective-permute-done.4.caches = bf16[4,1024,128]{2,1,0:T(8,128)(2,1)S(1)} collective-permute-done((bf16[4,1024,128]{2,1,0:T(8,128)(2,1)S(1)}, bf16[4,1024,128]{2,1,0:T(8,128)(2,1)S(1)}, u32[]{:S(2)}, u32[]{:S(2)}) %collective-permute-start.4) | collective-permute-done | bytes 1048608 | tf_op jit(solution)/shard_map/ppermute | solution.py:596
  129.3 1.9 %settle.1 = (bf16[2,1024,128]{2,1,0:T(8,128)(2,1)}, bf16[2,1024,128]{2,1,0:T(8,128)(2,1)}) custom-call(s32[32,128]{1,0:T(8,128)} %bitcast.20, s32[2,32]{1,0:T(2,128)} %bitcast.24, bf16[4,1024,128]{2,1,0:T(8,128)(2,1)S(1)} %collective-permute-done.4.caches), custom_call_target="tpu_custom_call" | custom-call | tf_op jit(solution)/shard_map/settle/pallas_call | solution.py:502
  131.2 0.0 all-to-all-done.1
  131.2 2.7 %combine.1 = bf16[32,2048]{1,0:T(8,128)(2,1)} custom-call(bf16[1024,1024]{1,0:T(8,128)(2,1)} %bitcast.9.ret_hbm, bf16[64,1024]{1,0:T(8,128)(2,1)S(1)} %get-tuple-element.41.high, bf16[64,1024]{1,0:T(8,128)(2,1)S(1)} %get-tuple-element.40.low, bf16[32,2048]{1,0:T(8,128)(2,1)S(1)} %get-tuple-element.21.hidden), custom_call_target="tpu_custom_call" | custom-call | tf_op jit(solution)/shard_map/combine/pallas_call | solution.py:543
  (8 shorter events, 0.1 us)
Async XLA Ops:
  0.6 12.8 %copy-start.4 = (s32[32,8]{0,1:T(8,128)S(1)}, s32[32,8]{0,1:T(8,128)}, u32[]{:S(2)}) copy-start(s32[32,8]{0,1:T(8,128)} %param.29) | copy-start | bytes 3076
  9.6 5.0 %collective-permute-start = (bf16[48,128]{1,0:T(8,128)(2,1)S(1)}, bf16[48,128]{1,0:T(8,128)(2,1)S(1)}, u32[]{:S(2)}, u32[]{:S(2)}) collective-permute-start(bf16[48,128]{1,0:T(8,128)(2,1)S(1)} %get-tuple-element.15), channel_id=1, source_target_pairs={{0,64},{4,68},{8,72},{12,76},{16,80},{20,84},{24,88},{28,92},{32,9... | collective-permute-start | bytes 36872 | tf_op jit(solution)/shard_map/ppermute | solution.py:595
  14.6 56.5 %copy-start.1 = (bf16[1,2048,768]{2,1,0:T(8,128)(2,1)S(1)}, bf16[1,2048,768]{2,1,0:T(8,128)(2,1)}, u32[]{:S(2)}) copy-start(bf16[1,2048,768]{2,1,0:T(8,128)(2,1)} %wu.1) | copy-start | bytes 9437188
  14.6 56.4 %copy-start.2 = (bf16[1,768,2048]{2,1,0:T(8,128)(2,1)S(1)}, bf16[1,768,2048]{2,1,0:T(8,128)(2,1)}, u32[]{:S(2)}) copy-start(bf16[1,768,2048]{2,1,0:T(8,128)(2,1)} %wd.1) | copy-start | bytes 9437188
  17.5 6.2 %collective-permute-start.1 = (bf16[32,2048]{1,0:T(8,128)(2,1)S(1)}, bf16[32,2048]{1,0:T(8,128)(2,1)S(1)}, u32[]{:S(2)}, u32[]{:S(2)}) collective-permute-start(bf16[32,2048]{1,0:T(8,128)(2,1)S(1)} %get-tuple-element.17), channel_id=1, source_target_pairs={{0,1},{1,2},{2,3},{3,0},{4,5},{5,6},{6,7},{7,4},{8,9},{9,10},{10,1... | collective-permute-start | bytes 393224 | tf_op jit(solution)/shard_map/ppermute | solution.py:600
  19.2 7.7 %collective-permute-start.2 = (bf16[32,2048]{1,0:T(8,128)(2,1)S(1)}, bf16[32,2048]{1,0:T(8,128)(2,1)S(1)}, u32[]{:S(2)}, u32[]{:S(2)}) collective-permute-start(bf16[32,2048]{1,0:T(8,128)(2,1)S(1)} %get-tuple-element.18), channel_id=1, source_target_pairs={{0,2},{1,3},{2,0},{3,1},{4,6},{5,7},{6,4},{7,5},{8,10},{9,11},{10,... | collective-permute-start | bytes 393224 | tf_op jit(solution)/shard_map/ppermute | solution.py:600
  22.5 5.0 %collective-permute-start.3 = (bf16[32,2048]{1,0:T(8,128)(2,1)S(1)}, bf16[32,2048]{1,0:T(8,128)(2,1)S(1)}, u32[]{:S(2)}, u32[]{:S(2)}) collective-permute-start(bf16[32,2048]{1,0:T(8,128)(2,1)S(1)} %get-tuple-element.19), channel_id=1, source_target_pairs={{0,3},{1,0},{2,1},{3,2},{4,7},{5,4},{6,5},{7,6},{8,11},{9,8},{10,9... | collective-permute-start | bytes 393224 | tf_op jit(solution)/shard_map/ppermute | solution.py:600
  29.3 41.8 %copy-start = (bf16[1,2048,768]{2,1,0:T(8,128)(2,1)S(1)}, bf16[1,2048,768]{2,1,0:T(8,128)(2,1)}, u32[]{:S(2)}) copy-start(bf16[1,2048,768]{2,1,0:T(8,128)(2,1)} %wg.1) | copy-start | bytes 9437188
  77.0 7.8 %copy-start.3 = (f32[32,8]{0,1:T(8,128)S(1)}, f32[32,8]{0,1:T(8,128)}, u32[]{:S(2)}) copy-start(f32[32,8]{0,1:T(8,128)} %param.30) | copy-start | bytes 3076
  77.0 54.2 %all-to-all-start.1 = ((bf16[128,8,1024]{2,1,0:T(8,128)(2,1)}), bf16[128,8,1024]{2,1,0:T(8,128)(2,1)}, u32[]{:S(2)}, u32[]{:S(2)}) async-start(bf16[128,8,1024]{2,1,0:T(8,128)(2,1)} %bitcast.8), calls=%async_computation.1 | async-start | bytes 4194304 | tf_op jit(solution)/shard_map/all_to_all | solution.py:637
  81.8 47.5 %collective-permute-start.4 = (bf16[4,1024,128]{2,1,0:T(8,128)(2,1)S(1)}, bf16[4,1024,128]{2,1,0:T(8,128)(2,1)S(1)}, u32[]{:S(2)}, u32[]{:S(2)}) collective-permute-start(bf16[4,1024,128]{2,1,0:T(8,128)(2,1)S(1)} %get-tuple-element.22), channel_id=1, source_target_pairs={{0,64},{4,68},{8,72},{12,76},{16,80},{20,84},{24,88},{28,92},{32,9... | collective-permute-start | bytes 3145736 | tf_op jit(solution)/shard_map/ppermute | solution.py:596
